TPU v7x, 256 devices: a whole 4x4x8 slice. The times are simulated.
256 devices in a mesh: rows: 16 (over y, x), mus: 16 (over z, core).
Axes of the slice: x: 4, y: 4, z: 8, core: 2. Of those that a mesh axis runs over, the one named last changes fastest.
Arguments:
- sketch_seed: int32 [1], replicated, may hold values from 0 to 46336
- angles: int32 [6, 12288], P(None, 'rows'), may hold values from 0 to 63
- lengths: float32 [304, 12288], P(None, 'rows'), may hold values from -6 to 6
Outputs:
- coefficients: float32 [304, 462], P('mus')
- residual: float32 [304, 12288], P('mus', 'rows')
All inputs are finite; a program needn't handle non-finite values.
Results may differ from a plain program's by a relative error of at most 0.0003.
Values sent between devices are 32-bit elements; how exact they have to be, the bound alone decides.
No kernel may reach another device: no remote copies, remote signals or barrier semaphores. Data moves between devices by JAX's collectives and lax.ppermute only.
A program may use at most 64 MiB of HBM per device.

v0:
```python
import math

import jax
import jax.numpy as jnp
from jax import lax
from jax.sharding import PartitionSpec as P

ANGLES = 6
DEGREE = 5
TERMS = 462
SKETCH = 2048
GRID = 64
ITERS = 3


modulus = 46337
epsilon = 1e-06


def mix_round(values):
    return (values * values + 7919) % modulus


def sketch_block(seed_value, row_ids, pose_ids):
    row_code = mix_round((row_ids * 389 + seed_value) % modulus)
    pose_code = (pose_ids % modulus * 13 + seed_value) % modulus
    hashed = mix_round(mix_round((row_code[:, None] * 3 + pose_code[None, :]) % modulus))
    return ((hashed.astype(jnp.float32) + 0.5) * (2.0 / modulus) - 1.0) * math.sqrt(3.0 / SKETCH)


def exponent_table():
    tuples = [[]]
    for angle in range(ANGLES):
        tuples = [
            prefix + [order]
            for prefix in tuples
            for order in range(DEGREE + 1)
            if sum(prefix) + order <= DEGREE
        ]
    return [[entry[angle] for entry in tuples] for angle in range(ANGLES)]


def legendre_basis(indices):
    position = (2.0 * indices.astype(jnp.float32) + 1.0) / GRID - 1.0
    polynomials = [jnp.ones_like(position), position]
    for order in range(1, DEGREE):
        polynomials.append(
            ((2 * order + 1) * position * polynomials[order] - order * polynomials[order - 1])
            / (order + 1)
        )
    exponents = exponent_table()
    degrees = jnp.arange(DEGREE + 1, dtype=jnp.int32)
    product = None
    for angle in range(ANGLES):
        legendre = jnp.stack(
            [math.sqrt(2 * order + 1) * polynomials[order][angle] for order in range(DEGREE + 1)]
        )
        selector = (
            jnp.asarray(exponents[angle], dtype=jnp.int32)[:, None] == degrees[None, :]
        ).astype(jnp.float32)
        factor = jnp.dot(selector, legendre, precision=lax.Precision.HIGHEST)
        product = factor if product is None else product * factor
    return product


def contract_last(left, right):
    return lax.dot_general(left, right, (((1,), (1,)), ((), ())), precision=lax.Precision.HIGHEST)


def contract_first(left, right):
    return lax.dot_general(left, right, (((0,), (0,)), ((), ())), precision=lax.Precision.HIGHEST)


def front_solve(factor_low, values):
    return jax.scipy.linalg.solve_triangular(factor_low, values, lower=True)


def back_solve(factor_low, values):
    return jax.scipy.linalg.solve_triangular(factor_low, values, lower=True, trans=1)


def per_device(sketch_seed, angles, lengths):
    rows_count = lax.axis_size("rows")
    mus_count = lax.axis_size("mus")
    row_rank = lax.axis_index("rows")
    mus_rank = lax.axis_index("mus")
    pose_dev = angles.shape[1]
    block_width = min(256, pose_dev)
    block_count = pose_dev // block_width
    basis_scale = 1.0 / math.sqrt(pose_dev * rows_count)
    muscle_dev = lengths.shape[0] // mus_count
    sketch_dev = SKETCH // mus_count
    seed_value = sketch_seed[0]
    sketch_ids = mus_rank * sketch_dev + jnp.arange(sketch_dev, dtype=jnp.int32)
    own_lengths = lax.dynamic_slice_in_dim(lengths, mus_rank * muscle_dev, muscle_dev, 0)

    def basis_at(offset):
        return (
            legendre_basis(lax.dynamic_slice_in_dim(angles, offset, block_width, 1)) * basis_scale
        )

    def sketch_step(block_index, sums):
        offset = block_index.astype(jnp.int32) * block_width
        basis_block = basis_at(offset)
        pose_ids = row_rank * pose_dev + offset + jnp.arange(block_width, dtype=jnp.int32)
        weights = sketch_block(seed_value, sketch_ids, pose_ids)
        length_block = lax.dynamic_slice_in_dim(lengths, offset, block_width, 1)
        return (
            sums[0] + contract_last(weights, basis_block),
            sums[1] + contract_last(weights, length_block),
        )

    initial = (
        jnp.zeros((sketch_dev, TERMS), jnp.float32),
        jnp.zeros((sketch_dev, lengths.shape[0]), jnp.float32),
    )
    part_a, part_b = lax.fori_loop(0, block_count, sketch_step, initial)
    summed_a, summed_b = lax.psum((part_a, part_b), "rows")
    gathered = lax.all_gather(summed_a, "mus", axis=0, tiled=True)
    gram_matrix = contract_first(gathered, gathered)
    projected = lax.psum_scatter(
        contract_first(summed_b, summed_a), "mus", scatter_dimension=0, tiled=True
    )
    factor_low = jnp.linalg.cholesky(gram_matrix)
    start_coef = back_solve(factor_low, front_solve(factor_low, projected.T))

    def sweep_poses(weight, previous, direction):

        def pose_step(block_index, state):
            fresh_rows, summed, squares = state
            offset = block_index.astype(jnp.int32) * block_width
            basis_block = basis_at(offset)
            fresh = weight[:, None] * lax.dynamic_slice_in_dim(
                previous, offset, block_width, 1
            ) + contract_first(direction, basis_block)
            fresh_rows = lax.dynamic_update_slice_in_dim(fresh_rows, fresh, offset, 1)
            squares = squares + jnp.sum(fresh * fresh, axis=1)
            return (fresh_rows, summed, squares)

        state_init = (
            jnp.zeros((muscle_dev, pose_dev), jnp.float32),
            jnp.zeros((TERMS, muscle_dev), jnp.float32),
            jnp.zeros((muscle_dev,), jnp.float32),
        )
        return lax.fori_loop(0, block_count, pose_step, state_init)

    def project_back(unit_rows):

        def back_step(block_index, summed):
            offset = block_index.astype(jnp.int32) * block_width
            basis_block = basis_at(offset)
            return summed + contract_last(
                basis_block, lax.dynamic_slice_in_dim(unit_rows, offset, block_width, 1)
            )

        return lax.fori_loop(0, block_count, back_step, jnp.zeros((TERMS, muscle_dev), jnp.float32))

    def advance(weight, previous, direction):
        fresh_rows, summed, squares = sweep_poses(weight, previous, direction)
        squares = lax.psum(squares, "rows")
        u_norm = jnp.sqrt(squares + epsilon)
        unit_rows = fresh_rows / u_norm[:, None]
        return (unit_rows, u_norm, lax.psum(project_back(unit_rows), "rows"))

    unit_rows, u_norm, summed = advance(
        jnp.ones((muscle_dev,), jnp.float32), own_lengths, -start_coef
    )
    q_terms = front_solve(factor_low, summed)
    v_norm = jnp.sqrt(jnp.sum(q_terms * q_terms, axis=0) + epsilon)
    v_terms = q_terms / v_norm[None, :]
    w_terms = v_terms
    phi_bar = u_norm
    rot_bar = v_norm
    y_terms = jnp.zeros((TERMS, muscle_dev), jnp.float32)
    for step_index in range(ITERS):
        unit_rows, u_norm, summed = advance(-v_norm, unit_rows, back_solve(factor_low, v_terms))
        q_terms = front_solve(factor_low, summed) - u_norm[None, :] * v_terms
        v_norm = jnp.sqrt(jnp.sum(q_terms * q_terms, axis=0) + epsilon)
        v_terms = q_terms / v_norm[None, :]
        rot_norm = jnp.sqrt(rot_bar * rot_bar + u_norm * u_norm)
        cosine = rot_bar / rot_norm
        sine_term = u_norm / rot_norm
        rot_theta = sine_term * v_norm
        rot_bar = -cosine * v_norm
        phi_now = cosine * phi_bar
        phi_bar = sine_term * phi_bar
        y_terms = y_terms + (phi_now / rot_norm)[None, :] * w_terms
        w_terms = v_terms - (rot_theta / rot_norm)[None, :] * w_terms
    coef_terms = start_coef + back_solve(factor_low, y_terms)
    final_state = sweep_poses(jnp.ones((muscle_dev,), jnp.float32), own_lengths, -coef_terms)
    return (coef_terms.T, final_state[0])


def solution(mesh):
    placed = (P(), P(None, "rows"), P(None, "rows"))
    return jax.shard_map(
        per_device,
        mesh=mesh,
        in_specs=placed,
        out_specs=(P("mus", None), P("mus", "rows")),
        check_vma=False,
    )
```

profile of v0, /device:TPU:34, one launch (start us, length us, event | category | flops | bytes accessed | tf_op | source)
XLA Modules:
  0.0 787.0 jit_solution(5798679744864818253)
XLA Ops:
  7.2 32.8 %while.188 = (s32[]{:T(128)}, f32[128,462]{0,1:T(8,128)S(1)}, f32[128,304]{0,1:T(8,128)S(1)}, s32[]{:T(128)}, s32[]{:T(128)}, /*index=5*/s32[6,768]{1,0:T(8,128)...) while((s32[]{:T(128)}, f32[128,462]{0,1:T(8,128)S(1)}, ...), condition=%wide.region_1.2_spmd.clone.clone, body=%wide.region_0.1_spmd.sunk.clone.clone.sunk | while | flops 355126528 | bytes 7012186 | solution.py:117
  40.9 96.8 %all-reduce.10.cloned.1.call-done = (f32[128,462]{0,1:T(8,128)}, f32[128,304]{0,1:T(8,128)}) async-done(((f32[128,462]{0,1:T(8,128)}, f32[128,304]{0,1:T(8,128)}), (f32[128,462]{0,1:T(8,128)}, f32[128,304]{0,1:T(8,128)})) %all-reduce.10.cloned.1.call-update) | async-done | bytes 392208 | tf_op jit(solution)/shard_map/psum | solution.py:118
  140.4 29.8 %fusion.2 = f32[24,462]{1,0:T(8,128)S(1)} fusion(f32[304,462]{1,0:T(8,128)S(1)} %fusion.354), kind=kCustom, calls=%all-reduce-scatter | all-reduce-scatter fusion | flops 177409 | bytes 607168
  170.2 1.9 collective-permute-start
  174.1 8.0 %collective-permute-start.2 = (f32[24,462]{1,0:T(8,128)S(1)}, f32[24,462]{1,0:T(8,128)S(1)}, u32[]{:S(2)}, u32[]{:S(2)}) collective-permute-start(f32[24,462]{1,0:T(8,128)S(1)} %fusion.2), channel_id=1, source_target_pairs={{0,3},{1,4},{2,5},{3,6},{4,7},{5,8},{6,9},{7,10},{8,11},{9,12},{10... | collective-permute-start | bytes 133064
  182.1 1.9 collective-permute-start.3
  186.0 3.0 all-gather.2.cloned.1.call-done
  189.0 9.0 %fusion.353 = f32[462,462]{1,0:T(8,128)S(1)} fusion(f32[2048,462]{0,1:T(8,128)} %all-gather.2.cloned.1.call-done), kind=kOutput, calls=%fused_computation.886 | convolution fusion | flops 5245599744 | bytes 4638480 | tf_op jit(solution)/shard_map/dot_general | solution.py:71
  198.5 11.7 %cholesky.105 = f32[128,128]{1,0:T(8,128)S(1)} custom-call(f32[128,128]{1,0:T(8,128)S(1)} %cholesky.272), custom_call_target="Cholesky" | custom-call | tf_op jit(solution)/shard_map/jit(cholesky)/cholesky | solution.py:124
  210.3 9.8 %custom-call.33 = f32[1,128,128]{1,2,0:T(8,128)S(1)} custom-call(f32[1,128,128]{2,1,0:T(8,128)S(1)} %get-tuple-element.3921), custom_call_target="InvertDiagBlocksLowerTriangular" | custom-call | tf_op jit(solution)/shard_map/jit(cholesky)/cholesky | solution.py:124
  220.9 11.7 %cholesky.219 = f32[128,128]{1,0:T(8,128)S(1)} custom-call(f32[128,128]{1,0:T(8,128)S(1)} %cholesky.276), custom_call_target="Cholesky" | custom-call | tf_op jit(solution)/shard_map/jit(cholesky)/cholesky | solution.py:124
  232.7 10.2 %custom-call.34 = f32[1,128,128]{1,2,0:T(8,128)S(1)} custom-call(f32[1,128,128]{2,1,0:T(8,128)S(1)} %get-tuple-element.3918), custom_call_target="InvertDiagBlocksLowerTriangular" | custom-call | tf_op jit(solution)/shard_map/jit(cholesky)/cholesky | solution.py:124
  243.5 11.7 %cholesky.240 = f32[128,128]{1,0:T(8,128)S(1)} custom-call(f32[128,128]{1,0:T(8,128)S(1)} %cholesky.281), custom_call_target="Cholesky" | custom-call | tf_op jit(solution)/shard_map/jit(cholesky)/cholesky | solution.py:124
  255.9 9.8 %custom-call.35 = f32[1,128,128]{1,2,0:T(8,128)S(1)} custom-call(f32[1,128,128]{2,1,0:T(8,128)S(1)} %get-tuple-element.3915), custom_call_target="InvertDiagBlocksLowerTriangular" | custom-call | tf_op jit(solution)/shard_map/jit(cholesky)/cholesky | solution.py:124
  266.2 7.1 cholesky.260
  277.5 6.0 while.196
  283.6 39.5 %custom-call.53 = f32[4,128,128]{1,2,0:T(8,128)S(1)} custom-call(f32[4,128,128]{2,1,0:T(8,128)S(1)} %pad_maximum_fusion), custom_call_target="InvertDiagBlocksLowerTriangular" | custom-call | tf_op jit(solution)/shard_map/jit(_solve_triangular)/triangular_solve | solution.py:79
  326.1 9.8 %while.189 = (s32[]{:T(128)}, f32[19,768]{1,0:T(8,128)S(1)}, f32[19]{0:T(128)S(1)}, f32[19,768]{1,0:T(8,128)S(1)}, s32[6,768]{1,0:T(8,128)S(1)}, /*index=5*/f32[...) while((s32[]{:T(128)}, f32[19,768]{1,0:T(8,128)S(1)}, ...), condition=%wide.region_15.18_spmd.clone.clone, body=%wide.region_13.17_spmd.sunk.clone.clone.sunk | while | flops 78866448 | bytes 6005525 | solution.py:145
  335.9 38.4 %psum.65 = f32[19]{0:T(128)S(1)} all-reduce(f32[19]{0:T(128)S(1)} %get-tuple-element.2848), channel_id=1, replica_groups=mesh['rows'=16,'mus'=16] {'rows'}, use_global_device_ids=true, to_apply=%region_16.19 | all-reduce | flops 19 | bytes 152 | tf_op jit(solution)/shard_map/psum | solution.py:160
  374.5 9.9 %while.190 = (s32[]{:T(128)}, f32[462,19]{0,1:T(8,128)S(1)}, s32[6,768]{1,0:T(8,128)S(1)}, f32[19,768]{1,0:T(8,128)S(1)}, s32[]{:T(128)}, /*index=5*/f32[]{:T(12...) while((s32[]{:T(128)}, f32[462,19]{0,1:T(8,128)S(1)}, ...), condition=%wide.region_18.21_spmd.clone.clone, body=%wide.region_17.20_spmd.sunk.clone.clone.sunk | while | flops 78869392 | bytes 6015305 | solution.py:156
  384.3 70.7 %psum.66 = f32[462,19]{0,1:T(8,128)S(1)} all-reduce(f32[462,19]{0,1:T(8,128)S(1)} %get-tuple-element.2849), channel_id=1, replica_groups=mesh['rows'=16,'mus'=16] {'rows'}, use_global_device_ids=true, to_apply=%region_19.22 | all-reduce | flops 8778 | bytes 70224 | tf_op jit(solution)/shard_map/psum | solution.py:163
  458.2 9.8 %while.191 = (s32[]{:T(128)}, f32[19,768]{1,0:T(8,128)S(1)}, f32[19]{0:T(128)S(1)}, f32[19]{0:T(128)S(1)}, f32[19,768]{1,0:T(8,128)S(1)}, /*index=5*/s32[6,768]{...) while((s32[]{:T(128)}, f32[19,768]{1,0:T(8,128)S(1)}, ...), condition=%wide.region_23.26_spmd.clone.clone, body=%wide.region_21.25_spmd.sunk.clone.clone.sunk | while | flops 78871312 | bytes 6006045 | solution.py:145
  468.0 39.1 %psum.67 = f32[19]{0:T(128)S(1)} all-reduce(f32[19]{0:T(128)S(1)} %get-tuple-element.2850), channel_id=1, replica_groups=mesh['rows'=16,'mus'=16] {'rows'}, use_global_device_ids=true, to_apply=%region_24.27 | all-reduce | flops 19 | bytes 152 | tf_op jit(solution)/shard_map/psum | solution.py:160
  507.3 9.9 %while.192 = (s32[]{:T(128)}, f32[462,19]{0,1:T(8,128)S(1)}, s32[6,768]{1,0:T(8,128)S(1)}, f32[19,768]{1,0:T(8,128)S(1)}, s32[]{:T(128)}, /*index=5*/f32[]{:T(12...) while((s32[]{:T(128)}, f32[462,19]{0,1:T(8,128)S(1)}, ...), condition=%wide.region_26.29_spmd.clone.clone, body=%wide.region_25.28_spmd.sunk.clone.clone.sunk | while | flops 78869392 | bytes 6015305 | solution.py:156
  517.1 66.2 %psum.68 = f32[462,19]{0,1:T(8,128)S(1)} all-reduce(f32[462,19]{0,1:T(8,128)S(1)} %get-tuple-element.2852), channel_id=1, replica_groups=mesh['rows'=16,'mus'=16] {'rows'}, use_global_device_ids=true, to_apply=%region_27.30 | all-reduce | flops 8778 | bytes 70224 | tf_op jit(solution)/shard_map/psum | solution.py:163
  586.6 9.8 %while.193 = (s32[]{:T(128)}, f32[19,768]{1,0:T(8,128)S(1)}, f32[19]{0:T(128)S(1)}, f32[19]{0:T(128)S(1)}, f32[19,768]{1,0:T(8,128)S(1)}, /*index=5*/s32[6,768]{...) while((s32[]{:T(128)}, f32[19,768]{1,0:T(8,128)S(1)}, ...), condition=%wide.region_31.34_spmd.clone.clone, body=%wide.region_29.33_spmd.sunk.clone.clone.sunk | while | flops 78871312 | bytes 6006045 | solution.py:145
  596.4 40.7 %psum.69 = f32[19]{0:T(128)S(1)} all-reduce(f32[19]{0:T(128)S(1)} %get-tuple-element.2853), channel_id=1, replica_groups=mesh['rows'=16,'mus'=16] {'rows'}, use_global_device_ids=true, to_apply=%region_32.35 | all-reduce | flops 19 | bytes 152 | tf_op jit(solution)/shard_map/psum | solution.py:160
  637.2 9.9 %while.194 = (s32[]{:T(128)}, f32[462,19]{0,1:T(8,128)S(1)}, s32[6,768]{1,0:T(8,128)S(1)}, f32[19,768]{1,0:T(8,128)S(1)}, s32[]{:T(128)}, /*index=5*/f32[]{:T(12...) while((s32[]{:T(128)}, f32[462,19]{0,1:T(8,128)S(1)}, ...), condition=%wide.region_34.37_spmd.clone.clone, body=%wide.region_33.36_spmd.sunk.clone.clone.sunk | while | flops 78869392 | bytes 6015305 | solution.py:156
  647.1 66.5 %psum.70 = f32[462,19]{0,1:T(8,128)S(1)} all-reduce(f32[462,19]{0,1:T(8,128)S(1)} %get-tuple-element.2855), channel_id=1, replica_groups=mesh['rows'=16,'mus'=16] {'rows'}, use_global_device_ids=true, to_apply=%region_35.38 | all-reduce | flops 8778 | bytes 70224 | tf_op jit(solution)/shard_map/psum | solution.py:163
  716.8 9.8 %while.195 = (s32[]{:T(128)}, f32[19]{0:T(128)S(1)}, f32[19]{0:T(128)S(1)}, f32[19,768]{1,0:T(8,128)S(1)}, s32[6,768]{1,0:T(8,128)S(1)}, /*index=5*/f32[462,19]{...) while((s32[]{:T(128)}, f32[19]{0:T(128)S(1)}, ...), condition=%wide.region_39.42_spmd.clone.clone, body=%wide.region_37.41_spmd.sunk.clone.clone.sunk | while | flops 78871312 | bytes 5959381 | solution.py:145
  726.6 40.8 %psum.71 = f32[19]{0:T(128)S(1)} all-reduce(f32[19]{0:T(128)S(1)} %get-tuple-element.2856), channel_id=1, replica_groups=mesh['rows'=16,'mus'=16] {'rows'}, use_global_device_ids=true, to_apply=%region_40.43 | all-reduce | flops 19 | bytes 152 | tf_op jit(solution)/shard_map/psum | solution.py:160
  769.7 9.4 %while.187 = (s32[]{:T(128)}, f32[19,768]{1,0:T(8,128)S(1)}, f32[19,768]{1,0:T(8,128)S(1)}, s32[6,768]{1,0:T(8,128)S(1)}, f32[462,19]{0,1:T(8,128)S(1)}, /*index...) while((s32[]{:T(128)}, f32[19,768]{1,0:T(8,128)S(1)}, ...), condition=%wide.region_42.45_spmd.clone, body=%wide.region_41.44_spmd.sunk.clone.sunk | while | flops 78856704 | bytes 6004767 | solution.py:145
  (713 shorter events, 140.3 us)
Async XLA Ops:
  7.2 130.6 %all-reduce.10.cloned.1.call-start = ((), (), s32[]{:S(2)}) async-start(), calls=%async_computation.1 | async-start | bytes 786432 | tf_op jit(solution)/shard_map/psum | solution.py:118
  7.2 176.9 %copy-start.11 = (u32[256]{0:T(256)S(1)}, u32[256]{0:T(256)}, u32[]{:S(2)}) copy-start(u32[256]{0:T(256)} %constant.2424) | copy-start | bytes 3076
  7.3 6.4 copy-start.6
  18.2 6.4 copy-start.6
  29.2 6.4 copy-start.6
  40.1 0.7 copy-start.8
  40.1 0.7 copy-start.9
  40.9 148.1 %all-gather.2.cloned.1.call-start = ((), (), s32[]{:S(2)}) async-start(), calls=%async_computation | async-start | bytes 4038656 | tf_op jit(solution)/shard_map/all_gather | solution.py:119
  170.2 15.1 %collective-permute-start = (f32[24,462]{1,0:T(8,128)S(1)}, f32[24,462]{1,0:T(8,128)S(1)}, u32[]{:S(2)}, u32[]{:S(2)}) collective-permute-start(f32[24,462]{1,0:T(8,128)S(1)} %fusion.2), channel_id=1, source_target_pairs={{0,1},{1,2},{2,3},{3,4},{4,5},{5,6},{6,7},{7,8},{8,9},{9,10},{10,1... | collective-permute-start | bytes 133064
  172.2 13.2 %collective-permute-start.1 = (f32[24,462]{1,0:T(8,128)S(1)}, f32[24,462]{1,0:T(8,128)S(1)}, u32[]{:S(2)}, u32[]{:S(2)}) collective-permute-start(f32[24,462]{1,0:T(8,128)S(1)} %fusion.2), channel_id=1, source_target_pairs={{0,2},{1,3},{2,4},{3,5},{4,6},{5,7},{6,8},{7,9},{8,10},{9,11},{10,... | collective-permute-start | bytes 133064
  174.1 11.3 %collective-permute-start.2 = (f32[24,462]{1,0:T(8,128)S(1)}, f32[24,462]{1,0:T(8,128)S(1)}, u32[]{:S(2)}, u32[]{:S(2)}) collective-permute-start(f32[24,462]{1,0:T(8,128)S(1)} %fusion.2), channel_id=1, source_target_pairs={{0,3},{1,4},{2,5},{3,6},{4,7},{5,8},{6,9},{7,10},{8,11},{9,12},{10... | collective-permute-start | bytes 133064
  182.1 3.3 collective-permute-start.3
  220.5 105.5 %copy-start = (s32[6,768]{1,0:T(8,128)S(1)}, s32[6,768]{1,0:T(8,128)}, u32[]{:S(2)}) copy-start(s32[6,768]{1,0:T(8,128)} %get-tuple-element.5395) | copy-start | bytes 55300
  220.5 105.5 %copy-start.1 = (s32[462]{0:T(512)S(1)}, s32[462]{0:T(512)}, u32[]{:S(2)}) copy-start(s32[462]{0:T(512)} %get-tuple-element.5403) | copy-start | bytes 5548
  220.5 105.5 %copy-start.2 = (s32[462]{0:T(512)S(1)}, s32[462]{0:T(512)}, u32[]{:S(2)}) copy-start(s32[462]{0:T(512)} %get-tuple-element.5411) | copy-start | bytes 5548
  220.5 105.5 %copy-start.3 = (s32[462]{0:T(512)S(1)}, s32[462]{0:T(512)}, u32[]{:S(2)}) copy-start(s32[462]{0:T(512)} %get-tuple-element.5419) | copy-start | bytes 5548
  220.6 105.5 %copy-start.4 = (s32[462]{0:T(512)S(1)}, s32[462]{0:T(512)}, u32[]{:S(2)}) copy-start(s32[462]{0:T(512)} %get-tuple-element.5427) | copy-start | bytes 5548
  220.6 105.5 %copy-start.5 = (s32[462]{0:T(512)S(1)}, s32[462]{0:T(512)}, u32[]{:S(2)}) copy-start(s32[462]{0:T(512)} %get-tuple-element.5435) | copy-start | bytes 5548
  220.6 105.5 %copy-start.7 = (s32[462]{0:T(512)S(1)}, s32[462]{0:T(512)}, u32[]{:S(2)}) copy-start(s32[462]{0:T(512)} %get-tuple-element.5443) | copy-start | bytes 5548
  779.1 0.6 copy-start.10
Sparse Core Ops, SparseCore 0:
  41.0 96.7 all-reduce.9
  139.5 49.4 all-gather.1
where the time goes:
time: 795 us; the launch traced here: 787 us
  blocking collectives  392 us (49%)
  other arithmetic  125 us (16%)
  matrix products  120 us (15%)
  waiting for transfers between devices  99.9 us (13%)
  between operations  19 us (2%)
  local copies, waits for them, and re-layouts  14.5 us (2%)
  starting transfers between devices  13.8 us (2%)
    psum x3, blocking collectives, advance(): return (unit_rows, u_norm, lax.psum(project_back(unit_rows), 'rows'))  203 us
    psum x4, blocking collectives, advance(): squares = lax.psum(squares, 'rows')  159 us
    psum x1, waiting for transfers between devices, per_device(): summed_a, summed_b = lax.psum((part_a, part_b), 'rows')  96.8 us
    dot_general x162, matrix products, legendre_basis(): factor = jnp.dot(selector, legendre, precision=lax.Precision.HIGHEST)  74.7 us
    another operation x14, other arithmetic, per_device(): factor_low = jnp.linalg.cholesky(gram_matrix)  74.2 us
    another operation x11, other arithmetic, back_solve(): jax.scipy.linalg.solve_triangular(factor_low, values, lower=True, trans=1)  39.8 us
    unnamed x1, blocking collectives  29.8 us
    dot_general x17, matrix products, contract_first(): lax.dot_general(left, right, (((0,), (0,)), ((), ())), precision=lax.Prec...  17.7 us
  transfers between devices with their start and end apart: 6, of which 2 were waited for; matrix products, arithmetic and copies ran while one was open for 4% of the time, Pallas kernels for 0%

commit v1 on v0

v1 whole, which is shorter than its diff:
```python
import functools
import math

import jax
import jax.numpy as jnp
import numpy as np
from jax import lax
from jax.experimental import pallas as pl
from jax.experimental.pallas import tpu as pltpu
from jax.sharding import PartitionSpec as P

ANGLES = 6
DEGREE = 5
TERMS = 462
MUSCLES = 304
SKETCH = 2048
GRID = 64
ITERS = 3
POSES = 12288

ROWS = 16
MUS = 16
POSE_DEV = POSES // ROWS
OWN = MUSCLES // MUS
SKETCH_DEV = SKETCH // MUS
PAD = 512
FIRST = 464
STACK = FIRST + MUSCLES
BLOCK = PAD // ROWS
PAIR = 32

modulus = 46337
epsilon = 1e-06

f32, bf16, i32 = jnp.float32, jnp.bfloat16, jnp.int32
HIGHEST = lax.Precision.HIGHEST
NN = (((1,), (0,)), ((), ()))
NT = (((1,), (1,)), ((), ()))
TN = (((0,), (0,)), ((), ()))


def exponent_table():
    tuples = [[]]
    for angle in range(ANGLES):
        tuples = [
            prefix + [order]
            for prefix in tuples
            for order in range(DEGREE + 1)
            if sum(prefix) + order <= DEGREE
        ]
    return tuples


PAIRS = [(i, j) for i in range(DEGREE + 1) for j in range(DEGREE + 1 - i)]


def pair_selectors():
    table = np.zeros((3, PAD, 3 * PAIR), np.float32)
    for j, entry in enumerate(exponent_table()):
        for g in range(3):
            at = PAIRS.index((entry[2 * g], entry[2 * g + 1]))
            for piece in range(3):
                table[g, j, piece * PAIR + at] = 1.0
    return table


def split2(x):
    high = x.astype(bf16)
    return high, (x - high.astype(f32)).astype(bf16)


def dot3(a, b, dims):
    (ah, al), (bh, bl) = a, b
    one = functools.partial(lax.dot_general, dimension_numbers=dims, preferred_element_type=f32)
    return one(ah, bh) + (one(ah, bl) + one(al, bh))


def exact(a, b, dims):
    return lax.dot_general(a, b, dims, precision=HIGHEST, preferred_element_type=f32)


def mod_m(x):
    quotient = (x.astype(f32) * (1.0 / modulus) - 0.01).astype(i32)
    rest = x - quotient * modulus
    return jnp.where(rest >= modulus, rest - modulus, rest)


def mix_round(x):
    return mod_m(x * x + 7919)


def local_kernel(sc_ref, ang_ref, len_ref, sel_ref, z_ref, basis_ref, own_ref, pair_ref, stack_ref, right_ref):
    row_rank, mus_rank, seed = sc_ref[0], sc_ref[1], sc_ref[2]
    position = (2.0 * ang_ref[...].astype(f32) + 1.0) / GRID - 1.0
    plain = [jnp.ones_like(position), position]
    for order in range(1, DEGREE):
        plain.append(
            ((2 * order + 1) * position * plain[order] - order * plain[order - 1])
            * (1.0 / (order + 1))
        )
    scaled = [math.sqrt(2 * order + 1) * plain[order] for order in range(DEGREE + 1)]
    pair_ref[...] = jnp.zeros_like(pair_ref)
    for g in range(3):
        for at, (i, j) in enumerate(PAIRS):
            pair_ref[g, at : at + 1, :] = (
                scaled[i][2 * g : 2 * g + 1] * scaled[j][2 * g + 1 : 2 * g + 2]
            )
    product = None
    for g in range(3):
        whole = pair_ref[g]
        high = whole.astype(bf16)
        rest = whole - high.astype(f32)
        mid = rest.astype(bf16)
        low = (rest - mid.astype(f32)).astype(bf16)
        pieces = jnp.concatenate([high, mid, low], axis=0)
        factor = lax.dot_general(sel_ref[g], pieces, NN, preferred_element_type=f32)
        product = factor if product is None else product * factor
    basis = product * (1.0 / math.sqrt(POSES))
    basis_ref[...] = basis
    stack_ref[0:FIRST, :] = basis[0:FIRST]
    stack_ref[FIRST:STACK, :] = len_ref[...]

    sketch_ids = mus_rank * SKETCH_DEV + lax.broadcasted_iota(i32, (SKETCH_DEV, 1), 0)
    pose_ids = row_rank * POSE_DEV + lax.broadcasted_iota(i32, (1, POSE_DEV), 1)
    row_code = mod_m(3 * mix_round(mod_m(sketch_ids * 389 + seed)))
    pose_code = mod_m(mod_m(pose_ids) * 13 + seed)
    code = row_code + pose_code
    code = jnp.where(code >= modulus, code - modulus, code)
    hashed = mix_round(mix_round(code))
    sketch = ((hashed.astype(f32) + 0.5) * (2.0 / modulus) - 1.0) * math.sqrt(3.0 / SKETCH)
    both = dot3(split2(sketch), split2(stack_ref[...]), NT)
    for r in range(ROWS):
        z_ref[r, :, 0:STACK] = both[8 * r : 8 * r + 8]

    own_ref[...] = jnp.zeros_like(own_ref)
    for k in range(OWN):
        own_ref[k : k + 1, :] = len_ref[pl.ds(mus_rank * OWN + k, 1), :]
    right_ref[0:BLOCK, :] = basis_ref[pl.ds(pl.multiple_of(mus_rank * BLOCK, BLOCK), BLOCK), :]
    right_ref[BLOCK : 2 * BLOCK, :] = own_ref[...]
    columns = dot3(split2(basis), split2(right_ref[...]), NT)
    own = own_ref[...]
    squares = exact(jnp.ones((8, POSE_DEV), f32), own * own, NT)
    for r in range(ROWS):
        for k in range(4):
            at = BLOCK * r + 8 * k
            z_ref[r, :, STACK + 64 * k : STACK + 64 * k + 64] = columns[at : at + 8]
    z_ref[ROWS - 1, :, STACK + 192 + BLOCK : STACK + 256] = squares


def gram_kernel(sc_ref, all_ref, out_ref, full_ref, place_ref):
    row_rank, mus_rank = sc_ref[0], sc_ref[1]
    both = jnp.concatenate([all_ref[r, :, 0:STACK] for r in range(ROWS)], axis=0)
    parts = split2(both)
    full_ref[...] = dot3((parts[0][:, 0:PAD], parts[1][:, 0:PAD]), parts, TN)
    out_ref[:, 0:STACK] = full_ref[pl.ds(pl.multiple_of(row_rank * BLOCK, BLOCK), BLOCK), :]
    place_ref[...] = jnp.zeros_like(place_ref)
    for k in range(4):
        place_ref[8 * k : 8 * k + 8, 0:BLOCK] = all_ref[
            row_rank, :, STACK + 64 * k : STACK + 64 * k + BLOCK
        ]
    out_ref[:, STACK : STACK + PAD] = pltpu.roll(place_ref[...], mus_rank * BLOCK, 1)


def solve_kernel(
    sc_ref, mine_ref, theirs_ref, all_ref, basis_ref, own_ref, coef_ref, res_ref,
    whole_ref, m_ref, x_ref, e_ref, c_ref,
):
    mus_rank = sc_ref[1]
    core = lax.rem(mus_rank, 2)
    half = BLOCK // 2

    def assemble(top_ref, bottom_ref):
        for r in range(ROWS):
            whole_ref[BLOCK * r : BLOCK * r + half, :] = top_ref[r]
            whole_ref[BLOCK * r + half : BLOCK * r + BLOCK, :] = bottom_ref[r]

    @pl.when(core == 0)
    def _():
        assemble(mine_ref, theirs_ref)

    @pl.when(core == 1)
    def _():
        assemble(theirs_ref, mine_ref)

    rows = lax.broadcasted_iota(i32, (PAD, PAD), 0)
    cols = lax.broadcasted_iota(i32, (PAD, PAD), 1)
    unit = (rows == cols).astype(f32)
    inside = (rows < TERMS) & (cols < TERMS)
    m_ref[...] = jnp.where(inside, whole_ref[:, 0:PAD], unit)
    c_ref[...] = jnp.zeros_like(c_ref)
    for r in range(ROWS):
        for k in range(4):
            at = BLOCK * r + 8 * k
            c_ref[at : at + 8, 0:BLOCK] = all_ref[
                r, :, STACK + 64 * k + BLOCK : STACK + 64 * k + 64
            ]
    c_all = c_ref[...]
    lengths2 = c_all[PAD - 1 : PAD, :]
    valid = lax.broadcasted_iota(i32, (PAD, 128), 0) < TERMS
    c_own = jnp.where(valid, c_all, 0.0)
    pick = (
        lax.broadcasted_iota(i32, (STACK - 384, 128), 0) + 384
        == lax.broadcasted_iota(i32, (STACK - 384, 128), 1) + FIRST + mus_rank * OWN
    ) & (lax.broadcasted_iota(i32, (STACK - 384, 128), 1) < OWN)
    projected = exact(whole_ref[:, 384:STACK], pick.astype(f32), NN)
    projected = jnp.where(valid, projected, 0.0)

    def plain(a, b):
        return lax.dot_general(a.astype(bf16), b.astype(bf16), NN, preferred_element_type=f32)

    gram = m_ref[...]
    frob = 1.0 / jnp.sqrt(jnp.sum(gram * gram))
    normed = gram * frob
    square = plain(normed, normed)
    fourth = plain(square, square)
    bound = jnp.sqrt(jnp.sqrt(jnp.sqrt(jnp.sum(fourth * fourth))))
    x_ref[...] = unit * (1.84 * frob / bound)

    def coarse(_, carry):
        x = x_ref[...]
        e = unit - plain(m_ref[...], x)
        x_ref[...] = x + plain(x, e)
        return carry

    lax.fori_loop(0, 5, coarse, 0)

    def fine(state):
        step, _ = state
        x = x_ref[...]
        e = unit - exact(m_ref[...], x, NN)
        x_ref[...] = x + plain(x, e)
        return step + 1, jnp.sum(e * e)

    lax.while_loop(lambda s: (s[0] < 40) & (s[1] > 1e-6), fine, (0, jnp.float32(1.0)))

    inv = functools.partial(lambda b: exact(x_ref[...], b, NN))
    e_ref[...] = jnp.where(inside, whole_ref[:, STACK : STACK + PAD], 0.0)
    apply_g = functools.partial(lambda b: exact(e_ref[...], b, NN))

    def total(a):
        return jnp.sum(a, axis=0, keepdims=True)

    start = inv(projected)
    g_start = apply_g(start)
    g_hat = c_own - g_start
    fresh2 = jnp.maximum(lengths2 - total(start * (c_own + g_hat)), 0.0)
    u_norm = jnp.sqrt(fresh2 + epsilon)
    g_hat = g_hat / u_norm
    u_square = fresh2 / (fresh2 + epsilon)
    t = inv(g_hat)
    v_norm = jnp.sqrt(jnp.maximum(total(g_hat * t), 0.0) + epsilon)
    v_hat = g_hat / v_norm
    t = t / v_norm
    w = t
    phi_bar = u_norm
    rot_bar = v_norm
    y = jnp.zeros_like(t)
    for step in range(ITERS):
        g_t = apply_g(t)
        fresh2 = jnp.maximum(
            total(t * (g_t - 2.0 * v_norm * g_hat)) + v_norm * v_norm * u_square, 0.0
        )
        u_norm = jnp.sqrt(fresh2 + epsilon)
        rot_norm = jnp.sqrt(rot_bar * rot_bar + u_norm * u_norm)
        cosine = rot_bar / rot_norm
        sine = u_norm / rot_norm
        y = y + (cosine * phi_bar / rot_norm) * w
        if step == ITERS - 1:
            break
        g_hat = (g_t - v_norm * g_hat) / u_norm
        u_square = fresh2 / (fresh2 + epsilon)
        q_hat = g_hat - u_norm * v_hat
        t = inv(q_hat)
        v_norm = jnp.sqrt(jnp.maximum(total(q_hat * t), 0.0) + epsilon)
        v_hat = q_hat / v_norm
        t = t / v_norm
        w = t - (sine * v_norm / rot_norm) * w
        rot_bar = -cosine * v_norm
        phi_bar = sine * phi_bar
    coef = jnp.transpose(start + y)
    coef_ref[...] = coef[0:OWN, 0:TERMS]
    fitted = exact(coef[0:BLOCK], basis_ref[...], NN)
    res_ref[...] = own_ref[0:OWN, :] - fitted[0:OWN]


def vmem():
    return pl.BlockSpec(memory_space=pltpu.VMEM)


def smem():
    return pl.BlockSpec(memory_space=pltpu.SMEM)


def per_device(sketch_seed, angles, lengths):
    row_rank = lax.axis_index("rows")
    mus_rank = lax.axis_index("mus")
    ranks = jnp.stack([row_rank, mus_rank, sketch_seed[0]]).astype(i32)
    selectors = jnp.asarray(pair_selectors(), dtype=bf16)

    z, basis, own = pl.pallas_call(
        local_kernel,
        out_shape=(
            jax.ShapeDtypeStruct((ROWS, 8, STACK + 256), f32),
            jax.ShapeDtypeStruct((PAD, POSE_DEV), f32),
            jax.ShapeDtypeStruct((BLOCK, POSE_DEV), f32),
        ),
        in_specs=[smem(), vmem(), vmem(), vmem()],
        out_specs=(vmem(), vmem(), vmem()),
        scratch_shapes=[
            pltpu.VMEM((3, PAIR, POSE_DEV), f32),
            pltpu.VMEM((STACK, POSE_DEV), f32),
            pltpu.VMEM((2 * BLOCK, POSE_DEV), f32),
        ],
        name="local_products",
    )(ranks, angles, lengths, selectors)

    summed = jnp.sum(lax.all_to_all(z, "rows", 0, 0), axis=0)
    everyone = lax.all_to_all(
        jnp.broadcast_to(summed[None], (ROWS,) + summed.shape), "rows", 0, 0
    )

    block = pl.pallas_call(
        gram_kernel,
        out_shape=jax.ShapeDtypeStruct((BLOCK, STACK + PAD), f32),
        in_specs=[smem(), vmem()],
        out_specs=vmem(),
        scratch_shapes=[pltpu.VMEM((PAD, STACK), f32), pltpu.VMEM((BLOCK, PAD), f32)],
        name="gram_block",
    )(ranks, everyone)

    for bit in (1, 2, 4, 8):
        block = block + lax.ppermute(block, "mus", [(i, i ^ bit) for i in range(MUS)])

    half = BLOCK // 2
    kept = jnp.where(lax.rem(mus_rank, 2) == 0, block[:half], block[half:])
    mine = lax.all_to_all(jnp.broadcast_to(kept[None], (ROWS,) + kept.shape), "rows", 0, 0)
    theirs = lax.ppermute(mine, "mus", [(i, i ^ 1) for i in range(MUS)])

    coef, residual = pl.pallas_call(
        solve_kernel,
        out_shape=(
            jax.ShapeDtypeStruct((OWN, TERMS), f32),
            jax.ShapeDtypeStruct((OWN, POSE_DEV), f32),
        ),
        in_specs=[smem()] + [vmem()] * 5,
        out_specs=(vmem(), vmem()),
        scratch_shapes=[
            pltpu.VMEM((PAD, STACK + PAD), f32),
            pltpu.VMEM((PAD, PAD), f32),
            pltpu.VMEM((PAD, PAD), f32),
            pltpu.VMEM((PAD, PAD), f32),
            pltpu.VMEM((PAD, 128), f32),
        ],
        name="solve",
    )(ranks, mine, theirs, everyone, basis, own)
    return coef, residual


def solution(mesh):
    placed = (P(), P(None, "rows"), P(None, "rows"))
    return jax.shard_map(
        per_device,
        mesh=mesh,
        in_specs=placed,
        out_specs=(P("mus", None), P("mus", "rows")),
        check_vma=False,
    )
```

time: 795 us -> 133 us (0.17)
  the two profiles are of different devices: /device:TPU:34 before, /device:TPU:1 now
where the time goes in v1:
time: 133 us; the launch traced here: 131 us
  blocking collectives  48.8 us (37%)
  Pallas kernels  39.4 us (30%)
  starting transfers between devices  19.9 us (15%)
  waiting for transfers between devices  18.8 us (14%)
  other arithmetic  1.6 us (1%)
  between operations  1.33 us (1%)
    pallas_call x1, Pallas kernels, per_device(): pl.pallas_call(solve_kernel, out_shape=(jax.ShapeDtypeStruct((OWN, TERMS)...  31.3 us
    all_to_all x1, blocking collectives, per_device(): summed = jnp.sum(lax.all_to_all(z, 'rows', 0, 0), axis=0)  18.1 us
    all_to_all x1, blocking collectives, per_device(): lax.all_to_all(jnp.broadcast_to(kept[None], (ROWS,) + kept.shape), 'rows'...  17.8 us
    ppermute x4, waiting for transfers between devices, per_device(): lax.ppermute(block, 'mus', [(i, i ^ bit) for i in range(MUS)])  16.1 us
    ppermute x4, starting transfers between devices, per_device(): lax.ppermute(block, 'mus', [(i, i ^ bit) for i in range(MUS)])  14.1 us
    all_to_all x1, blocking collectives, per_device(): lax.all_to_all(jnp.broadcast_to(summed[None], (ROWS,) + summed.shape), 'r...  13 us
    ppermute x1, starting transfers between devices, per_device(): theirs = lax.ppermute(mine, 'mus', [(i, i ^ 1) for i in range(MUS)])  5.85 us
    pallas_call x1, Pallas kernels, per_device(): pl.pallas_call(local_kernel, out_shape=(jax.ShapeDtypeStruct((ROWS, 8, ST...  5.55 us
  transfers between devices with their start and end apart: 5, of which 5 were waited for; matrix products, arithmetic and copies ran while one was open for 0% of the time, Pallas kernels for 0%

profile of v1, /device:TPU:1, one launch (start us, length us, event | category | flops | bytes accessed | tf_op | source)
XLA Modules:
  0.0 131.1 jit_solution(15386092476916563415)
XLA Ops:
  1.3 0.6 pad_add_fusion.sc_ref
  1.8 5.6 %local_products.1 = (f32[16,8,1024]{2,1,0:T(8,128)}, f32[512,768]{1,0:T(8,128)}, f32[32,768]{1,0:T(8,128)}) custom-call(s32[3]{0:T(128)} %pad_add_fusion.sc_ref, s32[6,768]{1,0:T(8,128)} %ang_ref.1, f32[304,768]{1,0:T(8,128)} %len_ref.1, bf16[3,512,96]{2,1,0:T(8,128)(2,1)} %constant.17.clone.sel_ref), custom_call_target="tpu_custom_call" | custom-call | tf_op jit(solution)/shard_map/local_products/pallas_call | solution.py:300
  7.4 18.1 %all_to_all.15 = f32[16,8,1024]{2,1,0:T(8,128)S(1)} all-to-all(f32[16,8,1024]{2,1,0:T(8,128)} %get-tuple-element.5), channel_id=1, replica_groups=mesh['rows'=16,'mus'=16] {'rows'}, dimensions={0} | all-to-all | bytes 1048576 | tf_op jit(solution)/shard_map/all_to_all | solution.py:317
  25.6 13.0 %all_to_all.16.all_ref = f32[16,8,1024]{2,1,0:T(8,128)} all-to-all(f32[16,8,1024]{2,1,0:T(8,128)S(1)} %broadcast_in_dim.4), channel_id=1, replica_groups=mesh['rows'=16,'mus'=16] {'rows'}, dimensions={0} | all-to-all | bytes 1048576 | tf_op jit(solution)/shard_map/all_to_all | solution.py:318
  38.5 2.5 %gram_block.1 = f32[32,1280]{1,0:T(8,128)} custom-call(s32[3]{0:T(128)} %pad_add_fusion.sc_ref, f32[16,8,1024]{2,1,0:T(8,128)} %all_to_all.16.all_ref), custom_call_target="tpu_custom_call" | custom-call | tf_op jit(solution)/shard_map/gram_block/pallas_call | solution.py:322
  41.1 2.8 %collective-permute-start = (f32[32,1280]{1,0:T(8,128)}, f32[32,1280]{1,0:T(8,128)S(1)}, u32[]{:S(2)}, u32[]{:S(2)}) collective-permute-start(f32[32,1280]{1,0:T(8,128)} %gram_block.1), channel_id=1, source_target_pairs={{0,1},{1,0},{2,3},{3,2},{4,5},{5,4},{6,7},{7,6},{8,9},{9,8},{10,11... | collective-permute-start | bytes 491528 | tf_op jit(solution)/shard_map/ppermute | solution.py:332
  43.9 1.2 collective-permute-done
  45.1 0.9 add.12
  46.1 1.7 %collective-permute-start.1 = (f32[32,1280]{1,0:T(8,128)S(1)}, f32[32,1280]{1,0:T(8,128)S(1)}, u32[]{:S(2)}, u32[]{:S(2)}) collective-permute-start(f32[32,1280]{1,0:T(8,128)S(1)} %add.12), channel_id=1, source_target_pairs={{0,2},{1,3},{2,0},{3,1},{4,6},{5,7},{6,4},{7,5},{8,10},{9,11},{10,... | collective-permute-start | bytes 491528 | tf_op jit(solution)/shard_map/ppermute | solution.py:332
  47.8 4.2 %collective-permute-done.1 = f32[32,1280]{1,0:T(8,128)S(1)} collective-permute-done((f32[32,1280]{1,0:T(8,128)S(1)}, f32[32,1280]{1,0:T(8,128)S(1)}, u32[]{:S(2)}, u32[]{:S(2)}) %collective-permute-start.1) | collective-permute-done | bytes 163872 | tf_op jit(solution)/shard_map/ppermute | solution.py:332
  52.0 3.1 %collective-permute-start.2 = (f32[32,1280]{1,0:T(8,128)S(1)}, f32[32,1280]{1,0:T(8,128)S(1)}, u32[]{:S(2)}, u32[]{:S(2)}) collective-permute-start(f32[32,1280]{1,0:T(8,128)S(1)} %add.13), channel_id=1, source_target_pairs={{0,4},{1,5},{2,6},{3,7},{4,0},{5,1},{6,2},{7,3},{8,12},{9,13},{10,... | collective-permute-start | bytes 491528 | tf_op jit(solution)/shard_map/ppermute | solution.py:332
  55.1 7.2 %collective-permute-done.2 = f32[32,1280]{1,0:T(8,128)S(1)} collective-permute-done((f32[32,1280]{1,0:T(8,128)S(1)}, f32[32,1280]{1,0:T(8,128)S(1)}, u32[]{:S(2)}, u32[]{:S(2)}) %collective-permute-start.2) | collective-permute-done | bytes 163872 | tf_op jit(solution)/shard_map/ppermute | solution.py:332
  62.3 6.4 %collective-permute-start.3 = (f32[32,1280]{1,0:T(8,128)S(1)}, f32[32,1280]{1,0:T(8,128)S(1)}, u32[]{:S(2)}, u32[]{:S(2)}) collective-permute-start(f32[32,1280]{1,0:T(8,128)S(1)} %add.14), channel_id=1, source_target_pairs={{0,8},{1,9},{2,10},{3,11},{4,12},{5,13},{6,14},{7,15},{8,0},{9,1},... | collective-permute-start | bytes 491528 | tf_op jit(solution)/shard_map/ppermute | solution.py:332
  68.7 3.5 %collective-permute-done.3 = f32[32,1280]{1,0:T(8,128)S(1)} collective-permute-done((f32[32,1280]{1,0:T(8,128)S(1)}, f32[32,1280]{1,0:T(8,128)S(1)}, u32[]{:S(2)}, u32[]{:S(2)}) %collective-permute-start.3) | collective-permute-done | bytes 163872 | tf_op jit(solution)/shard_map/ppermute | solution.py:332
  72.3 0.1 broadcast_in_dim.5
  72.4 17.8 %all_to_all.17.mine_ref = f32[16,16,1280]{2,1,0:T(8,128)S(1)} all-to-all(f32[16,16,1280]{2,1,0:T(8,128)S(1)} %broadcast_in_dim.5), channel_id=1, replica_groups=mesh['rows'=16,'mus'=16] {'rows'}, dimensions={0} | all-to-all | bytes 2621440 | tf_op jit(solution)/shard_map/all_to_all | solution.py:336
  90.2 0.0 copy-start
  90.2 5.9 %collective-permute-start.4 = (f32[16,16,1280]{2,1,0:T(8,128)S(1)}, f32[16,16,1280]{2,1,0:T(8,128)S(1)}, u32[]{:S(2)}, u32[]{:S(2)}) collective-permute-start(f32[16,16,1280]{2,1,0:T(8,128)S(1)} %all_to_all.17.mine_ref), channel_id=1, source_target_pairs={{0,1},{1,0},{2,3},{3,2},{4,5},{5,4},{6,7},{7,6},{8,9},{9,8},{10,11... | collective-permute-start | bytes 3932168 | tf_op jit(solution)/shard_map/ppermute | solution.py:337
  96.0 2.7 %collective-permute-done.4.theirs_ref = f32[16,16,1280]{2,1,0:T(8,128)S(1)} collective-permute-done((f32[16,16,1280]{2,1,0:T(8,128)S(1)}, f32[16,16,1280]{2,1,0:T(8,128)S(1)}, u32[]{:S(2)}, u32[]{:S(2)}) %collective-permute-start.4) | collective-permute-done | bytes 1310752 | tf_op jit(solution)/shard_map/ppermute | solution.py:337
  98.7 0.0 copy-start.1
  98.7 0.0 copy-done
  98.7 1.1 copy-done.1
  99.8 31.3 %solve.1 = (f32[19,462]{1,0:T(8,128)}, f32[19,768]{1,0:T(8,128)}) custom-call(s32[3]{0:T(128)} %pad_add_fusion.sc_ref, f32[16,16,1280]{2,1,0:T(8,128)} %copy-done, f32[16,16,1280]{2,1,0:T(8,128)} %copy-done.1, f32[16,8,1024]{2,1,0:T(8,128)} %all_to_all.16.all_ref, f32[512,768]{1,0:T(8,128)} %get-tuple-element.6.basis_ref, f32[32,768]{1,0:T(8,128)} %get-tuple-element.7.own_ref), custom_call_target="tpu_custom_call" | custom-call | tf_op jit(solution)/shard_map/solve/pallas_call | solution.py:339
  (6 shorter events, 0.1 us)
Async XLA Ops:
  41.1 4.1 %collective-permute-start = (f32[32,1280]{1,0:T(8,128)}, f32[32,1280]{1,0:T(8,128)S(1)}, u32[]{:S(2)}, u32[]{:S(2)}) collective-permute-start(f32[32,1280]{1,0:T(8,128)} %gram_block.1), channel_id=1, source_target_pairs={{0,1},{1,0},{2,3},{3,2},{4,5},{5,4},{6,7},{7,6},{8,9},{9,8},{10,11... | collective-permute-start | bytes 491528 | tf_op jit(solution)/shard_map/ppermute | solution.py:332
  46.1 5.9 %collective-permute-start.1 = (f32[32,1280]{1,0:T(8,128)S(1)}, f32[32,1280]{1,0:T(8,128)S(1)}, u32[]{:S(2)}, u32[]{:S(2)}) collective-permute-start(f32[32,1280]{1,0:T(8,128)S(1)} %add.12), channel_id=1, source_target_pairs={{0,2},{1,3},{2,0},{3,1},{4,6},{5,7},{6,4},{7,5},{8,10},{9,11},{10,... | collective-permute-start | bytes 491528 | tf_op jit(solution)/shard_map/ppermute | solution.py:332
  52.0 10.3 %collective-permute-start.2 = (f32[32,1280]{1,0:T(8,128)S(1)}, f32[32,1280]{1,0:T(8,128)S(1)}, u32[]{:S(2)}, u32[]{:S(2)}) collective-permute-start(f32[32,1280]{1,0:T(8,128)S(1)} %add.13), channel_id=1, source_target_pairs={{0,4},{1,5},{2,6},{3,7},{4,0},{5,1},{6,2},{7,3},{8,12},{9,13},{10,... | collective-permute-start | bytes 491528 | tf_op jit(solution)/shard_map/ppermute | solution.py:332
  62.3 10.0 %collective-permute-start.3 = (f32[32,1280]{1,0:T(8,128)S(1)}, f32[32,1280]{1,0:T(8,128)S(1)}, u32[]{:S(2)}, u32[]{:S(2)}) collective-permute-start(f32[32,1280]{1,0:T(8,128)S(1)} %add.14), channel_id=1, source_target_pairs={{0,8},{1,9},{2,10},{3,11},{4,12},{5,13},{6,14},{7,15},{8,0},{9,1},... | collective-permute-start | bytes 491528 | tf_op jit(solution)/shard_map/ppermute | solution.py:332
  90.2 8.5 %copy-start = (f32[16,16,1280]{2,1,0:T(8,128)}, f32[16,16,1280]{2,1,0:T(8,128)S(1)}, u32[]{:S(2)}) copy-start(f32[16,16,1280]{2,1,0:T(8,128)S(1)} %all_to_all.17.mine_ref) | copy-start | bytes 3932164
  90.2 8.5 %collective-permute-start.4 = (f32[16,16,1280]{2,1,0:T(8,128)S(1)}, f32[16,16,1280]{2,1,0:T(8,128)S(1)}, u32[]{:S(2)}, u32[]{:S(2)}) collective-permute-start(f32[16,16,1280]{2,1,0:T(8,128)S(1)} %all_to_all.17.mine_ref), channel_id=1, source_target_pairs={{0,1},{1,0},{2,3},{3,2},{4,5},{5,4},{6,7},{7,6},{8,9},{9,8},{10,11... | collective-permute-start | bytes 3932168 | tf_op jit(solution)/shard_map/ppermute | solution.py:337
  98.7 1.1 copy-start.1

commit v2 on v1

--- a/solution.py
+++ b/solution.py
@@ -143,27 +143,46 @@
     for r in range(ROWS):
         for k in range(4):
             at = BLOCK * r + 8 * k
-            z_ref[r, :, STACK + 64 * k : STACK + 64 * k + 64] = columns[at : at + 8]
-    z_ref[ROWS - 1, :, STACK + 192 + BLOCK : STACK + 256] = squares
-
-
-def gram_kernel(sc_ref, all_ref, out_ref, full_ref, place_ref):
-    row_rank, mus_rank = sc_ref[0], sc_ref[1]
+            lane = STACK + BLOCK * k
+            z_ref[r, :, lane : lane + BLOCK] = columns[at : at + 8, 0:BLOCK]
+            z_ref[r, :, lane + 128 : lane + 128 + BLOCK] = columns[at : at + 8, BLOCK:]
+    z_ref[ROWS - 1, :, STACK + 256 - BLOCK : STACK + 256] = squares
+
+
+def gram_kernel(sc_ref, all_ref, out_ref):
+    row_rank = sc_ref[0]
     both = jnp.concatenate([all_ref[r, :, 0:STACK] for r in range(ROWS)], axis=0)
-    parts = split2(both)
-    full_ref[...] = dot3((parts[0][:, 0:PAD], parts[1][:, 0:PAD]), parts, TN)
-    out_ref[:, 0:STACK] = full_ref[pl.ds(pl.multiple_of(row_rank * BLOCK, BLOCK), BLOCK), :]
-    place_ref[...] = jnp.zeros_like(place_ref)
-    for k in range(4):
-        place_ref[8 * k : 8 * k + 8, 0:BLOCK] = all_ref[
-            row_rank, :, STACK + 64 * k : STACK + 64 * k + BLOCK
-        ]
-    out_ref[:, STACK : STACK + PAD] = pltpu.roll(place_ref[...], mus_rank * BLOCK, 1)
+    turned = pltpu.roll(both[:, 0:PAD], lax.rem(PAD - row_rank * BLOCK, PAD), 1)
+    block = dot3(split2(turned[:, 0:128]), split2(both), TN)
+    out_ref[...] = jnp.zeros_like(out_ref)
+    for m in range(MUS):
+        for k in range(4):
+            rows = block[8 * k : 8 * k + 8]
+            lane = BLOCK * k
+            muscle = FIRST + OWN * m
+            out_ref[m, :, lane : lane + BLOCK] = rows[:, BLOCK * m : BLOCK * m + BLOCK]
+            out_ref[m, :, lane + 128 : lane + 128 + OWN] = rows[:, muscle : muscle + OWN]
+
+
+def place_kernel(sc_ref, tiles_ref, own_ref, out_ref, row_ref):
+    for m in range(MUS):
+        for k in range(4):
+            at = BLOCK * m
+            lane = BLOCK * k
+            row_ref[8 * k : 8 * k + 8, at : at + BLOCK] = tiles_ref[m, :, lane : lane + BLOCK]
+            row_ref[8 * k : 8 * k + 8, PAD + at : PAD + at + BLOCK] = tiles_ref[
+                m, :, lane + 128 : lane + 128 + BLOCK
+            ]
+    half = BLOCK // 2
+    core = lax.rem(sc_ref[1], 2)
+    out_ref[:, 0 : 2 * PAD] = row_ref[pl.ds(pl.multiple_of(core * half, half), half), :]
+    out_ref[0:8, 2 * PAD :] = own_ref[:, 128:256]
+    out_ref[8:half, 2 * PAD :] = jnp.zeros((half - 8, 128), f32)
 
 
 def solve_kernel(
     sc_ref, mine_ref, theirs_ref, all_ref, basis_ref, own_ref, coef_ref, res_ref,
-    whole_ref, m_ref, x_ref, e_ref, c_ref,
+    whole_ref, m_ref, x_ref, e_ref, c_ref, p_ref,
 ):
     mus_rank = sc_ref[1]
     core = lax.rem(mus_rank, 2)
@@ -171,8 +190,8 @@
 
     def assemble(top_ref, bottom_ref):
         for r in range(ROWS):
-            whole_ref[BLOCK * r : BLOCK * r + half, :] = top_ref[r]
-            whole_ref[BLOCK * r + half : BLOCK * r + BLOCK, :] = bottom_ref[r]
+            whole_ref[BLOCK * r : BLOCK * r + half, :] = top_ref[r, :, 0 : 2 * PAD]
+            whole_ref[BLOCK * r + half : BLOCK * r + BLOCK, :] = bottom_ref[r, :, 0 : 2 * PAD]
 
     @pl.when(core == 0)
     def _():
@@ -188,22 +207,22 @@
     inside = (rows < TERMS) & (cols < TERMS)
     m_ref[...] = jnp.where(inside, whole_ref[:, 0:PAD], unit)
     c_ref[...] = jnp.zeros_like(c_ref)
+    p_ref[...] = jnp.zeros_like(p_ref)
     for r in range(ROWS):
         for k in range(4):
             at = BLOCK * r + 8 * k
+            lane = BLOCK * k
             c_ref[at : at + 8, 0:BLOCK] = all_ref[
-                r, :, STACK + 64 * k + BLOCK : STACK + 64 * k + 64
+                r, :, STACK + 128 + lane : STACK + 128 + lane + BLOCK
+            ]
+            p_ref[at : at + 8, 0:BLOCK] = mine_ref[
+                r, 0:8, 2 * PAD + lane : 2 * PAD + lane + BLOCK
             ]
     c_all = c_ref[...]
     lengths2 = c_all[PAD - 1 : PAD, :]
     valid = lax.broadcasted_iota(i32, (PAD, 128), 0) < TERMS
     c_own = jnp.where(valid, c_all, 0.0)
-    pick = (
-        lax.broadcasted_iota(i32, (STACK - 384, 128), 0) + 384
-        == lax.broadcasted_iota(i32, (STACK - 384, 128), 1) + FIRST + mus_rank * OWN
-    ) & (lax.broadcasted_iota(i32, (STACK - 384, 128), 1) < OWN)
-    projected = exact(whole_ref[:, 384:STACK], pick.astype(f32), NN)
-    projected = jnp.where(valid, projected, 0.0)
+    projected = jnp.where(valid, p_ref[...], 0.0)
 
     def plain(a, b):
         return lax.dot_general(a.astype(bf16), b.astype(bf16), NN, preferred_element_type=f32)
@@ -234,7 +253,7 @@
     lax.while_loop(lambda s: (s[0] < 40) & (s[1] > 1e-6), fine, (0, jnp.float32(1.0)))
 
     inv = functools.partial(lambda b: exact(x_ref[...], b, NN))
-    e_ref[...] = jnp.where(inside, whole_ref[:, STACK : STACK + PAD], 0.0)
+    e_ref[...] = jnp.where(inside, whole_ref[:, PAD : 2 * PAD], 0.0)
     apply_g = functools.partial(lambda b: exact(e_ref[...], b, NN))
 
     def total(a):
@@ -319,20 +338,26 @@
         jnp.broadcast_to(summed[None], (ROWS,) + summed.shape), "rows", 0, 0
     )
 
-    block = pl.pallas_call(
+    parts = pl.pallas_call(
         gram_kernel,
-        out_shape=jax.ShapeDtypeStruct((BLOCK, STACK + PAD), f32),
+        out_shape=jax.ShapeDtypeStruct((MUS, 8, 256), f32),
         in_specs=[smem(), vmem()],
         out_specs=vmem(),
-        scratch_shapes=[pltpu.VMEM((PAD, STACK), f32), pltpu.VMEM((BLOCK, PAD), f32)],
         name="gram_block",
     )(ranks, everyone)
-
-    for bit in (1, 2, 4, 8):
-        block = block + lax.ppermute(block, "mus", [(i, i ^ bit) for i in range(MUS)])
+    tile = jnp.sum(lax.all_to_all(parts, "mus", 0, 0), axis=0)
+    send = jnp.concatenate([tile[:, 0:128], summed[:, STACK : STACK + 128]], axis=1)
+    tiles = lax.all_to_all(jnp.broadcast_to(send[None], (MUS,) + send.shape), "mus", 0, 0)
 
     half = BLOCK // 2
-    kept = jnp.where(lax.rem(mus_rank, 2) == 0, block[:half], block[half:])
+    kept = pl.pallas_call(
+        place_kernel,
+        out_shape=jax.ShapeDtypeStruct((half, 2 * PAD + 128), f32),
+        in_specs=[smem(), vmem(), vmem()],
+        out_specs=vmem(),
+        scratch_shapes=[pltpu.VMEM((BLOCK, 2 * PAD), f32)],
+        name="place_rows",
+    )(ranks, tiles, tile)
     mine = lax.all_to_all(jnp.broadcast_to(kept[None], (ROWS,) + kept.shape), "rows", 0, 0)
     theirs = lax.ppermute(mine, "mus", [(i, i ^ 1) for i in range(MUS)])
 
@@ -345,10 +370,11 @@
         in_specs=[smem()] + [vmem()] * 5,
         out_specs=(vmem(), vmem()),
         scratch_shapes=[
-            pltpu.VMEM((PAD, STACK + PAD), f32),
+            pltpu.VMEM((PAD, 2 * PAD), f32),
             pltpu.VMEM((PAD, PAD), f32),
             pltpu.VMEM((PAD, PAD), f32),
             pltpu.VMEM((PAD, PAD), f32),
+            pltpu.VMEM((PAD, 128), f32),
             pltpu.VMEM((PAD, 128), f32),
         ],
         name="solve",

time: 133 us -> 134 us (level)
  blocking collectives: 48.8 us -> 63.8 us
  starting transfers between devices: 19.9 us -> 12.4 us
  waiting for transfers between devices: 18.8 us -> 11.6 us
    ppermute x4 -> x0, waiting for transfers between devices: 16.1 us -> none  [per_device(): lax.ppermute(block, 'mus', [(i, i ^ bit) for i in range(MUS)])]
    ppermute x4 -> x0, starting transfers between devices: 14.1 us -> none  [per_device(): lax.ppermute(block, 'mus', [(i, i ^ bit) for i in range(MUS)])]
    all_to_all x0 -> x1, blocking collectives: none -> 11.7 us  [per_device(): lax.all_to_all(jnp.broadcast_to(send[None], (MUS,) + send.shape), 'mus',...]
    all_to_all x0 -> x1, starting transfers between devices: none -> 11.3 us  [per_device(): tile = jnp.sum(lax.all_to_all(parts, 'mus', 0, 0), axis=0)]
    all_to_all x0 -> x1, waiting for transfers between devices: none -> 9.16 us  [per_device(): tile = jnp.sum(lax.all_to_all(parts, 'mus', 0, 0), axis=0)]
    ppermute x1, starting transfers between devices: 5.85 us -> 1.08 us  [per_device(): theirs = lax.ppermute(mine, 'mus', [(i, i ^ 1) for i in range(MUS)])]
    all_to_all x1, blocking collectives: 17.8 us -> 21.1 us  [per_device(): lax.all_to_all(jnp.broadcast_to(kept[None], (ROWS,) + kept.shape), 'rows'...]
    pallas_call x1 -> x2, Pallas kernels: 2.53 us -> 4.05 us  [the longest x1 2.33 us: per_device(): pl.pallas_call(gram_kernel, out_shape=jax.ShapeDtypeStruct((MUS, 8, 256),...]
  transfers between devices with their start and end apart: 5 -> 2, of which waited for: 5 -> 2; matrix products, arithmetic and copies ran while one was open for 0% -> 0% of each run, Pallas kernels for 0% -> 0%
where the time goes in v2:
time: 134 us; the launch traced here: 132 us
  blocking collectives  63.8 us (48%)
  Pallas kernels  40.5 us (30%)
  starting transfers between devices  12.4 us (9%)
  waiting for transfers between devices  11.6 us (9%)
  local copies, waits for them, and re-layouts  2.05 us (2%)
  between operations  1.34 us (1%)
    pallas_call x1, Pallas kernels, per_device(): pl.pallas_call(solve_kernel, out_shape=(jax.ShapeDtypeStruct((OWN, TERMS)...  30.9 us
    all_to_all x1, blocking collectives, per_device(): lax.all_to_all(jnp.broadcast_to(kept[None], (ROWS,) + kept.shape), 'rows'...  21.1 us
    all_to_all x1, blocking collectives, per_device(): summed = jnp.sum(lax.all_to_all(z, 'rows', 0, 0), axis=0)  18.1 us
    all_to_all x1, blocking collectives, per_device(): lax.all_to_all(jnp.broadcast_to(summed[None], (ROWS,) + summed.shape), 'r...  13 us
    all_to_all x1, blocking collectives, per_device(): lax.all_to_all(jnp.broadcast_to(send[None], (MUS,) + send.shape), 'mus',...  11.7 us
    all_to_all x1, starting transfers between devices, per_device(): tile = jnp.sum(lax.all_to_all(parts, 'mus', 0, 0), axis=0)  11.3 us
    all_to_all x1, waiting for transfers between devices, per_device(): tile = jnp.sum(lax.all_to_all(parts, 'mus', 0, 0), axis=0)  9.16 us
    pallas_call x1, Pallas kernels, per_device(): pl.pallas_call(local_kernel, out_shape=(jax.ShapeDtypeStruct((ROWS, 8, ST...  5.57 us
  transfers between devices with their start and end apart: 2, of which 2 were waited for; matrix products, arithmetic and copies ran while one was open for 0% of the time, Pallas kernels for 0%

profile of v2, /device:TPU:1, one launch (start us, length us, event | category | flops | bytes accessed | tf_op | source)
XLA Modules:
  0.0 132.4 jit_solution(6989835714226795926)
XLA Ops:
  1.3 0.6 pad_add_fusion.sc_ref
  1.9 5.6 %local_products.1 = (f32[16,8,1024]{2,1,0:T(8,128)}, f32[512,768]{1,0:T(8,128)}, f32[32,768]{1,0:T(8,128)}) custom-call(s32[3]{0:T(128)} %pad_add_fusion.sc_ref, s32[6,768]{1,0:T(8,128)} %ang_ref.1, f32[304,768]{1,0:T(8,128)} %len_ref.1, bf16[3,512,96]{2,1,0:T(8,128)(2,1)} %constant.11.clone.sel_ref), custom_call_target="tpu_custom_call" | custom-call | tf_op jit(solution)/shard_map/local_products/pallas_call | solution.py:319
  7.4 18.1 %all_to_all.25 = f32[16,8,1024]{2,1,0:T(8,128)S(1)} all-to-all(f32[16,8,1024]{2,1,0:T(8,128)} %get-tuple-element.5), channel_id=1, replica_groups=mesh['rows'=16,'mus'=16] {'rows'}, dimensions={0} | all-to-all | bytes 1048576 | tf_op jit(solution)/shard_map/all_to_all | solution.py:336
  25.6 13.0 %all_to_all.26.all_ref = f32[16,8,1024]{2,1,0:T(8,128)} all-to-all(f32[16,8,1024]{2,1,0:T(8,128)S(1)} %broadcast_in_dim.6), channel_id=1, replica_groups=mesh['rows'=16,'mus'=16] {'rows'}, dimensions={0} | all-to-all | bytes 1048576 | tf_op jit(solution)/shard_map/all_to_all | solution.py:337
  38.6 2.3 %gram_block.1 = f32[16,8,256]{2,1,0:T(8,128)} custom-call(s32[3]{0:T(128)} %pad_add_fusion.sc_ref, f32[16,8,1024]{2,1,0:T(8,128)} %all_to_all.26.all_ref), custom_call_target="tpu_custom_call" | custom-call | tf_op jit(solution)/shard_map/gram_block/pallas_call | solution.py:341
  40.9 11.3 %all-to-all-start.2 = ((f32[16,8,256]{2,1,0:T(8,128)}), f32[16,8,256]{2,1,0:T(8,128)S(1)}, u32[]{:S(2)}, u32[]{:S(2)}) async-start(f32[16,8,256]{2,1,0:T(8,128)} %gram_block.1), calls=%async_computation.2 | async-start | bytes 262144 | tf_op jit(solution)/shard_map/all_to_all | solution.py:348
  52.2 9.2 %all-to-all-done.2 = f32[16,8,256]{2,1,0:T(8,128)S(1)} async-done(((f32[16,8,256]{2,1,0:T(8,128)}), f32[16,8,256]{2,1,0:T(8,128)S(1)}, u32[]{:S(2)}, u32[]{:S(2)}) %all-to-all-start.2) | async-done | bytes 131104 | tf_op jit(solution)/shard_map/all_to_all | solution.py:348
  61.4 0.0 copy-start.2
  61.4 11.7 %all_to_all.27.tiles_ref = f32[16,8,256]{2,1,0:T(8,128)} all-to-all(f32[16,8,256]{2,1,0:T(8,128)S(1)} %broadcast_in_dim.7), channel_id=1, replica_groups=mesh['rows'=16,'mus'=16] {'mus'}, dimensions={0} | all-to-all | bytes 262144 | tf_op jit(solution)/shard_map/all_to_all | solution.py:350
  73.1 0.0 copy-done.2
  73.1 1.7 %place_rows.1 = f32[16,1152]{1,0:T(8,128)} custom-call(s32[3]{0:T(128)} %pad_add_fusion.sc_ref, f32[16,8,256]{2,1,0:T(8,128)} %all_to_all.27.tiles_ref, f32[8,256]{1,0:T(8,128)} %copy-done.2), custom_call_target="tpu_custom_call" | custom-call | tf_op jit(solution)/shard_map/place_rows/pallas_call | solution.py:353
  74.9 1.0 broadcast_in_dim.8
  75.8 21.1 %all_to_all.28.mine_ref = f32[16,16,1152]{2,1,0:T(8,128)S(1)} all-to-all(f32[16,16,1152]{2,1,0:T(8,128)S(1)} %broadcast_in_dim.8), channel_id=1, replica_groups=mesh['rows'=16,'mus'=16] {'rows'}, dimensions={0} | all-to-all | bytes 2359296 | tf_op jit(solution)/shard_map/all_to_all | solution.py:361
  96.9 0.0 copy-start
  96.9 1.1 collective-permute-start
  98.0 2.5 %collective-permute-done.theirs_ref = f32[16,16,1152]{2,1,0:T(8,128)S(1)} collective-permute-done((f32[16,16,1152]{2,1,0:T(8,128)S(1)}, f32[16,16,1152]{2,1,0:T(8,128)S(1)}, u32[]{:S(2)}, u32[]{:S(2)}) %collective-permute-start) | collective-permute-done | bytes 1179680 | tf_op jit(solution)/shard_map/ppermute | solution.py:362
  100.5 0.0 copy-start.1
  100.5 0.0 copy-done
  100.5 1.0 copy-done.1
  101.5 30.9 %solve.1 = (f32[19,462]{1,0:T(8,128)}, f32[19,768]{1,0:T(8,128)}) custom-call(s32[3]{0:T(128)} %pad_add_fusion.sc_ref, f32[16,16,1152]{2,1,0:T(8,128)} %copy-done, f32[16,16,1152]{2,1,0:T(8,128)} %copy-done.1, f32[16,8,1024]{2,1,0:T(8,128)} %all_to_all.26.all_ref, f32[512,768]{1,0:T(8,128)} %get-tuple-element.6.basis_ref, f32[32,768]{1,0:T(8,128)} %get-tuple-element.7.own_ref), custom_call_target="tpu_custom_call" | custom-call | tf_op jit(solution)/shard_map/solve/pallas_call | solution.py:364
  (7 shorter events, 0.1 us)
Async XLA Ops:
  40.9 20.5 %all-to-all-start.2 = ((f32[16,8,256]{2,1,0:T(8,128)}), f32[16,8,256]{2,1,0:T(8,128)S(1)}, u32[]{:S(2)}, u32[]{:S(2)}) async-start(f32[16,8,256]{2,1,0:T(8,128)} %gram_block.1), calls=%async_computation.2 | async-start | bytes 262144 | tf_op jit(solution)/shard_map/all_to_all | solution.py:348
  61.4 11.7 %copy-start.2 = (f32[8,256]{1,0:T(8,128)}, f32[8,256]{1,0:T(8,128)S(1)}, u32[]{:S(2)}) copy-start(f32[8,256]{1,0:T(8,128)S(1)} %reduce_sum.19.own_ref) | copy-start | bytes 24580
  96.9 3.6 %copy-start = (f32[16,16,1152]{2,1,0:T(8,128)}, f32[16,16,1152]{2,1,0:T(8,128)S(1)}, u32[]{:S(2)}) copy-start(f32[16,16,1152]{2,1,0:T(8,128)S(1)} %all_to_all.28.mine_ref) | copy-start | bytes 3538948
  96.9 3.5 %collective-permute-start = (f32[16,16,1152]{2,1,0:T(8,128)S(1)}, f32[16,16,1152]{2,1,0:T(8,128)S(1)}, u32[]{:S(2)}, u32[]{:S(2)}) collective-permute-start(f32[16,16,1152]{2,1,0:T(8,128)S(1)} %all_to_all.28.mine_ref), channel_id=1, source_target_pairs={{0,1},{1,0},{2,3},{3,2},{4,5},{5,4},{6,7},{7,6},{8,9},{9,8},{10,11... | collective-permute-start | bytes 3538952 | tf_op jit(solution)/shard_map/ppermute | solution.py:362
  100.5 1.0 copy-start.1

commit v3 on v2

--- a/solution.py
+++ b/solution.py
@@ -182,7 +182,7 @@
 
 def solve_kernel(
     sc_ref, mine_ref, theirs_ref, all_ref, basis_ref, own_ref, coef_ref, res_ref,
-    whole_ref, m_ref, x_ref, e_ref, c_ref, p_ref,
+    whole_ref, x_ref, mh_ref, ml_ref, xh_ref, xl_ref, gh_ref, gl_ref, c_ref, p_ref,
 ):
     mus_rank = sc_ref[1]
     core = lax.rem(mus_rank, 2)
@@ -205,7 +205,9 @@
     cols = lax.broadcasted_iota(i32, (PAD, PAD), 1)
     unit = (rows == cols).astype(f32)
     inside = (rows < TERMS) & (cols < TERMS)
-    m_ref[...] = jnp.where(inside, whole_ref[:, 0:PAD], unit)
+    gram = jnp.where(inside, whole_ref[:, 0:PAD], unit)
+    mh_ref[...], ml_ref[...] = split2(gram)
+    gh_ref[...], gl_ref[...] = split2(jnp.where(inside, whole_ref[:, PAD : 2 * PAD], 0.0))
     c_ref[...] = jnp.zeros_like(c_ref)
     p_ref[...] = jnp.zeros_like(p_ref)
     for r in range(ROWS):
@@ -227,34 +229,45 @@
     def plain(a, b):
         return lax.dot_general(a.astype(bf16), b.astype(bf16), NN, preferred_element_type=f32)
 
-    gram = m_ref[...]
     frob = 1.0 / jnp.sqrt(jnp.sum(gram * gram))
-    normed = gram * frob
+    normed = (gram * frob).astype(bf16)
     square = plain(normed, normed)
     fourth = plain(square, square)
     bound = jnp.sqrt(jnp.sqrt(jnp.sqrt(jnp.sum(fourth * fourth))))
-    x_ref[...] = unit * (1.84 * frob / bound)
+    scale = 1.84 * frob / bound
+    x_ref[...] = (2.0 * scale) * unit - (scale * scale) * gram
 
     def coarse(_, carry):
         x = x_ref[...]
-        e = unit - plain(m_ref[...], x)
-        x_ref[...] = x + plain(x, e)
+        high = x.astype(bf16)
+        e = unit - plain(mh_ref[...], high)
+        x_ref[...] = x + plain(high, e)
         return carry
 
-    lax.fori_loop(0, 5, coarse, 0)
+    lax.fori_loop(0, 4, coarse, 0)
 
     def fine(state):
         step, _ = state
         x = x_ref[...]
-        e = unit - exact(m_ref[...], x, NN)
-        x_ref[...] = x + plain(x, e)
+        parts = split2(x)
+        e = unit - dot3((mh_ref[...], ml_ref[...]), parts, NN)
+        x_ref[...] = x + plain(parts[0], e)
         return step + 1, jnp.sum(e * e)
 
     lax.while_loop(lambda s: (s[0] < 40) & (s[1] > 1e-6), fine, (0, jnp.float32(1.0)))
-
-    inv = functools.partial(lambda b: exact(x_ref[...], b, NN))
-    e_ref[...] = jnp.where(inside, whole_ref[:, PAD : 2 * PAD], 0.0)
-    apply_g = functools.partial(lambda b: exact(e_ref[...], b, NN))
+    xh_ref[...], xl_ref[...] = split2(x_ref[...])
+
+    left = lax.broadcasted_iota(i32, (PAD, 128), 1) < 64
+
+    def times(high_ref, low_ref, b):
+        high = b.astype(bf16).astype(f32)
+        pieces = jnp.where(left, high, pltpu.roll(b - high, 64, 1)).astype(bf16)
+        one = functools.partial(lax.dot_general, dimension_numbers=NN, preferred_element_type=f32)
+        product = one(high_ref[...], pieces) + one(low_ref[...], pieces)
+        return product + pltpu.roll(product, 64, 1)
+
+    inv = functools.partial(times, xh_ref, xl_ref)
+    apply_g = functools.partial(times, gh_ref, gl_ref)
 
     def total(a):
         return jnp.sum(a, axis=0, keepdims=True)
@@ -298,7 +311,7 @@
         phi_bar = sine * phi_bar
     coef = jnp.transpose(start + y)
     coef_ref[...] = coef[0:OWN, 0:TERMS]
-    fitted = exact(coef[0:BLOCK], basis_ref[...], NN)
+    fitted = dot3(split2(coef[0:BLOCK]), split2(basis_ref[...]), NN)
     res_ref[...] = own_ref[0:OWN, :] - fitted[0:OWN]
 
 
@@ -372,8 +385,9 @@
         scratch_shapes=[
             pltpu.VMEM((PAD, 2 * PAD), f32),
             pltpu.VMEM((PAD, PAD), f32),
-            pltpu.VMEM((PAD, PAD), f32),
-            pltpu.VMEM((PAD, PAD), f32),
+        ]
+        + [pltpu.VMEM((PAD, PAD), bf16)] * 6
+        + [
             pltpu.VMEM((PAD, 128), f32),
             pltpu.VMEM((PAD, 128), f32),
         ],

time: 134 us -> 122 us (0.910)
  Pallas kernels: 40.5 us -> 29.6 us
    pallas_call x1, Pallas kernels: 30.9 us -> 20 us  [per_device(): pl.pallas_call(solve_kernel, out_shape=(jax.ShapeDtypeStruct((OWN, TERMS)...]
where the time goes in v3:
time: 122 us; the launch traced here: 121 us
  blocking collectives  63.8 us (52%)
  Pallas kernels  29.6 us (24%)
  starting transfers between devices  12.4 us (10%)
  waiting for transfers between devices  11.6 us (10%)
  local copies, waits for them, and re-layouts  2.05 us (2%)
  between operations  1.34 us (1%)
    all_to_all x1, blocking collectives, per_device(): lax.all_to_all(jnp.broadcast_to(kept[None], (ROWS,) + kept.shape), 'rows'...  21.1 us
    pallas_call x1, Pallas kernels, per_device(): pl.pallas_call(solve_kernel, out_shape=(jax.ShapeDtypeStruct((OWN, TERMS)...  20 us
    all_to_all x1, blocking collectives, per_device(): summed = jnp.sum(lax.all_to_all(z, 'rows', 0, 0), axis=0)  18.1 us
    all_to_all x1, blocking collectives, per_device(): lax.all_to_all(jnp.broadcast_to(summed[None], (ROWS,) + summed.shape), 'r...  13 us
    all_to_all x1, blocking collectives, per_device(): lax.all_to_all(jnp.broadcast_to(send[None], (MUS,) + send.shape), 'mus',...  11.7 us
    all_to_all x1, starting transfers between devices, per_device(): tile = jnp.sum(lax.all_to_all(parts, 'mus', 0, 0), axis=0)  11.3 us
    all_to_all x1, waiting for transfers between devices, per_device(): tile = jnp.sum(lax.all_to_all(parts, 'mus', 0, 0), axis=0)  9.16 us
    pallas_call x1, Pallas kernels, per_device(): pl.pallas_call(local_kernel, out_shape=(jax.ShapeDtypeStruct((ROWS, 8, ST...  5.57 us
  transfers between devices with their start and end apart: 2, of which 2 were waited for; matrix products, arithmetic and copies ran while one was open for 0% of the time, Pallas kernels for 0%

profile of v3, /device:TPU:1, one launch (start us, length us, event | category | flops | bytes accessed | tf_op | source)
XLA Modules:
  0.0 121.5 jit_solution(5078877221037663612)
XLA Ops:
  1.3 0.6 pad_add_fusion.sc_ref
  1.9 5.6 %local_products.1 = (f32[16,8,1024]{2,1,0:T(8,128)}, f32[512,768]{1,0:T(8,128)}, f32[32,768]{1,0:T(8,128)}) custom-call(s32[3]{0:T(128)} %pad_add_fusion.sc_ref, s32[6,768]{1,0:T(8,128)} %ang_ref.1, f32[304,768]{1,0:T(8,128)} %len_ref.1, bf16[3,512,96]{2,1,0:T(8,128)(2,1)} %constant.11.clone.sel_ref), custom_call_target="tpu_custom_call" | custom-call | tf_op jit(solution)/shard_map/local_products/pallas_call | solution.py:332
  7.4 18.1 %all_to_all.25 = f32[16,8,1024]{2,1,0:T(8,128)S(1)} all-to-all(f32[16,8,1024]{2,1,0:T(8,128)} %get-tuple-element.5), channel_id=1, replica_groups=mesh['rows'=16,'mus'=16] {'rows'}, dimensions={0} | all-to-all | bytes 1048576 | tf_op jit(solution)/shard_map/all_to_all | solution.py:349
  25.6 13.0 %all_to_all.26.all_ref = f32[16,8,1024]{2,1,0:T(8,128)} all-to-all(f32[16,8,1024]{2,1,0:T(8,128)S(1)} %broadcast_in_dim.6), channel_id=1, replica_groups=mesh['rows'=16,'mus'=16] {'rows'}, dimensions={0} | all-to-all | bytes 1048576 | tf_op jit(solution)/shard_map/all_to_all | solution.py:350
  38.6 2.3 %gram_block.1 = f32[16,8,256]{2,1,0:T(8,128)} custom-call(s32[3]{0:T(128)} %pad_add_fusion.sc_ref, f32[16,8,1024]{2,1,0:T(8,128)} %all_to_all.26.all_ref), custom_call_target="tpu_custom_call" | custom-call | tf_op jit(solution)/shard_map/gram_block/pallas_call | solution.py:354
  40.9 11.3 %all-to-all-start.2 = ((f32[16,8,256]{2,1,0:T(8,128)}), f32[16,8,256]{2,1,0:T(8,128)S(1)}, u32[]{:S(2)}, u32[]{:S(2)}) async-start(f32[16,8,256]{2,1,0:T(8,128)} %gram_block.1), calls=%async_computation.2 | async-start | bytes 262144 | tf_op jit(solution)/shard_map/all_to_all | solution.py:361
  52.2 9.2 %all-to-all-done.2 = f32[16,8,256]{2,1,0:T(8,128)S(1)} async-done(((f32[16,8,256]{2,1,0:T(8,128)}), f32[16,8,256]{2,1,0:T(8,128)S(1)}, u32[]{:S(2)}, u32[]{:S(2)}) %all-to-all-start.2) | async-done | bytes 131104 | tf_op jit(solution)/shard_map/all_to_all | solution.py:361
  61.4 0.0 copy-start.2
  61.4 11.7 %all_to_all.27.tiles_ref = f32[16,8,256]{2,1,0:T(8,128)} all-to-all(f32[16,8,256]{2,1,0:T(8,128)S(1)} %broadcast_in_dim.7), channel_id=1, replica_groups=mesh['rows'=16,'mus'=16] {'mus'}, dimensions={0} | all-to-all | bytes 262144 | tf_op jit(solution)/shard_map/all_to_all | solution.py:363
  73.1 0.0 copy-done.2
  73.1 1.7 %place_rows.1 = f32[16,1152]{1,0:T(8,128)} custom-call(s32[3]{0:T(128)} %pad_add_fusion.sc_ref, f32[16,8,256]{2,1,0:T(8,128)} %all_to_all.27.tiles_ref, f32[8,256]{1,0:T(8,128)} %copy-done.2), custom_call_target="tpu_custom_call" | custom-call | tf_op jit(solution)/shard_map/place_rows/pallas_call | solution.py:366
  74.9 1.0 broadcast_in_dim.8
  75.8 21.1 %all_to_all.28.mine_ref = f32[16,16,1152]{2,1,0:T(8,128)S(1)} all-to-all(f32[16,16,1152]{2,1,0:T(8,128)S(1)} %broadcast_in_dim.8), channel_id=1, replica_groups=mesh['rows'=16,'mus'=16] {'rows'}, dimensions={0} | all-to-all | bytes 2359296 | tf_op jit(solution)/shard_map/all_to_all | solution.py:374
  96.9 0.0 copy-start
  96.9 1.1 collective-permute-start
  98.0 2.5 %collective-permute-done.theirs_ref = f32[16,16,1152]{2,1,0:T(8,128)S(1)} collective-permute-done((f32[16,16,1152]{2,1,0:T(8,128)S(1)}, f32[16,16,1152]{2,1,0:T(8,128)S(1)}, u32[]{:S(2)}, u32[]{:S(2)}) %collective-permute-start) | collective-permute-done | bytes 1179680 | tf_op jit(solution)/shard_map/ppermute | solution.py:375
  100.5 0.0 copy-start.1
  100.5 0.0 copy-done
  100.5 1.0 copy-done.1
  101.5 20.0 %solve.1 = (f32[19,462]{1,0:T(8,128)}, f32[19,768]{1,0:T(8,128)}) custom-call(s32[3]{0:T(128)} %pad_add_fusion.sc_ref, f32[16,16,1152]{2,1,0:T(8,128)} %copy-done, f32[16,16,1152]{2,1,0:T(8,128)} %copy-done.1, f32[16,8,1024]{2,1,0:T(8,128)} %all_to_all.26.all_ref, f32[512,768]{1,0:T(8,128)} %get-tuple-element.6.basis_ref, f32[32,768]{1,0:T(8,128)} %get-tuple-element.7.own_ref), custom_call_target="tpu_custom_call" | custom-call | tf_op jit(solution)/shard_map/solve/pallas_call | solution.py:377
  (7 shorter events, 0.1 us)
Async XLA Ops:
  40.9 20.5 %all-to-all-start.2 = ((f32[16,8,256]{2,1,0:T(8,128)}), f32[16,8,256]{2,1,0:T(8,128)S(1)}, u32[]{:S(2)}, u32[]{:S(2)}) async-start(f32[16,8,256]{2,1,0:T(8,128)} %gram_block.1), calls=%async_computation.2 | async-start | bytes 262144 | tf_op jit(solution)/shard_map/all_to_all | solution.py:361
  61.4 11.7 %copy-start.2 = (f32[8,256]{1,0:T(8,128)}, f32[8,256]{1,0:T(8,128)S(1)}, u32[]{:S(2)}) copy-start(f32[8,256]{1,0:T(8,128)S(1)} %reduce_sum.19.own_ref) | copy-start | bytes 24580
  96.9 3.6 %copy-start = (f32[16,16,1152]{2,1,0:T(8,128)}, f32[16,16,1152]{2,1,0:T(8,128)S(1)}, u32[]{:S(2)}) copy-start(f32[16,16,1152]{2,1,0:T(8,128)S(1)} %all_to_all.28.mine_ref) | copy-start | bytes 3538948
  96.9 3.5 %collective-permute-start = (f32[16,16,1152]{2,1,0:T(8,128)S(1)}, f32[16,16,1152]{2,1,0:T(8,128)S(1)}, u32[]{:S(2)}, u32[]{:S(2)}) collective-permute-start(f32[16,16,1152]{2,1,0:T(8,128)S(1)} %all_to_all.28.mine_ref), channel_id=1, source_target_pairs={{0,1},{1,0},{2,3},{3,2},{4,5},{5,4},{6,7},{7,6},{8,9},{9,8},{10,11... | collective-permute-start | bytes 3538952 | tf_op jit(solution)/shard_map/ppermute | solution.py:375
  100.5 1.0 copy-start.1

commit v4 on v3

--- a/solution.py
+++ b/solution.py
@@ -89,8 +89,8 @@
     return mod_m(x * x + 7919)
 
 
-def local_kernel(sc_ref, ang_ref, len_ref, sel_ref, z_ref, basis_ref, own_ref, pair_ref, stack_ref, right_ref):
-    row_rank, mus_rank, seed = sc_ref[0], sc_ref[1], sc_ref[2]
+def local_kernel(seed_ref, ang_ref, len_ref, sel_ref, z_ref, basis_ref, own_ref, pair_ref, stack_ref, right_ref):
+    row_rank, mus_rank, seed = lax.axis_index("rows"), lax.axis_index("mus"), seed_ref[0]
     position = (2.0 * ang_ref[...].astype(f32) + 1.0) / GRID - 1.0
     plain = [jnp.ones_like(position), position]
     for order in range(1, DEGREE):
@@ -149,8 +149,8 @@
     z_ref[ROWS - 1, :, STACK + 256 - BLOCK : STACK + 256] = squares
 
 
-def gram_kernel(sc_ref, all_ref, out_ref):
-    row_rank = sc_ref[0]
+def gram_kernel(all_ref, out_ref):
+    row_rank = lax.axis_index("rows")
     both = jnp.concatenate([all_ref[r, :, 0:STACK] for r in range(ROWS)], axis=0)
     turned = pltpu.roll(both[:, 0:PAD], lax.rem(PAD - row_rank * BLOCK, PAD), 1)
     block = dot3(split2(turned[:, 0:128]), split2(both), TN)
@@ -164,7 +164,7 @@
             out_ref[m, :, lane + 128 : lane + 128 + OWN] = rows[:, muscle : muscle + OWN]
 
 
-def place_kernel(sc_ref, tiles_ref, own_ref, out_ref, row_ref):
+def place_kernel(tiles_ref, own_ref, out_ref, row_ref):
     for m in range(MUS):
         for k in range(4):
             at = BLOCK * m
@@ -174,18 +174,21 @@
                 m, :, lane + 128 : lane + 128 + BLOCK
             ]
     half = BLOCK // 2
-    core = lax.rem(sc_ref[1], 2)
-    out_ref[:, 0 : 2 * PAD] = row_ref[pl.ds(pl.multiple_of(core * half, half), half), :]
-    out_ref[0:8, 2 * PAD :] = own_ref[:, 128:256]
-    out_ref[8:half, 2 * PAD :] = jnp.zeros((half - 8, 128), f32)
+    core = lax.rem(lax.axis_index("mus"), 2)
+    kept = row_ref[pl.ds(pl.multiple_of(core * half, half), half), :]
+    for r in range(ROWS):
+        out_ref[r, :, 0 : 2 * PAD] = kept
+        out_ref[r, 0:8, 2 * PAD :] = own_ref[:, 128:256]
+        out_ref[r, 8:half, 2 * PAD :] = jnp.zeros((half - 8, 128), f32)
 
 
 def solve_kernel(
-    sc_ref, mine_ref, theirs_ref, all_ref, basis_ref, own_ref, coef_ref, res_ref,
-    whole_ref, x_ref, mh_ref, ml_ref, xh_ref, xl_ref, gh_ref, gl_ref, c_ref, p_ref,
+    mine_ref, theirs_ref, all_ref, basis_hbm, own_ref, coef_ref, res_ref,
+    whole_ref, x_ref, mh_ref, ml_ref, xh_ref, xl_ref, gh_ref, gl_ref, c_ref, p_ref, basis_ref, sem,
 ):
-    mus_rank = sc_ref[1]
-    core = lax.rem(mus_rank, 2)
+    fetch = pltpu.make_async_copy(basis_hbm, basis_ref, sem)
+    fetch.start()
+    core = lax.rem(lax.axis_index("mus"), 2)
     half = BLOCK // 2
 
     def assemble(top_ref, bottom_ref):
@@ -215,7 +218,7 @@
             at = BLOCK * r + 8 * k
             lane = BLOCK * k
             c_ref[at : at + 8, 0:BLOCK] = all_ref[
-                r, :, STACK + 128 + lane : STACK + 128 + lane + BLOCK
+                r, :, STACK + lane : STACK + lane + BLOCK
             ]
             p_ref[at : at + 8, 0:BLOCK] = mine_ref[
                 r, 0:8, 2 * PAD + lane : 2 * PAD + lane + BLOCK
@@ -311,6 +314,7 @@
         phi_bar = sine * phi_bar
     coef = jnp.transpose(start + y)
     coef_ref[...] = coef[0:OWN, 0:TERMS]
+    fetch.wait()
     fitted = dot3(split2(coef[0:BLOCK]), split2(basis_ref[...]), NN)
     res_ref[...] = own_ref[0:OWN, :] - fitted[0:OWN]
 
@@ -324,9 +328,6 @@
 
 
 def per_device(sketch_seed, angles, lengths):
-    row_rank = lax.axis_index("rows")
-    mus_rank = lax.axis_index("mus")
-    ranks = jnp.stack([row_rank, mus_rank, sketch_seed[0]]).astype(i32)
     selectors = jnp.asarray(pair_selectors(), dtype=bf16)
 
     z, basis, own = pl.pallas_call(
@@ -344,20 +345,21 @@
             pltpu.VMEM((2 * BLOCK, POSE_DEV), f32),
         ],
         name="local_products",
-    )(ranks, angles, lengths, selectors)
+    )(sketch_seed, angles, lengths, selectors)
 
     summed = jnp.sum(lax.all_to_all(z, "rows", 0, 0), axis=0)
+    shared = jnp.concatenate([summed[:, 0:STACK], summed[:, STACK + 128 :]], axis=1)
     everyone = lax.all_to_all(
-        jnp.broadcast_to(summed[None], (ROWS,) + summed.shape), "rows", 0, 0
+        jnp.broadcast_to(shared[None], (ROWS,) + shared.shape), "rows", 0, 0
     )
 
     parts = pl.pallas_call(
         gram_kernel,
         out_shape=jax.ShapeDtypeStruct((MUS, 8, 256), f32),
-        in_specs=[smem(), vmem()],
+        in_specs=[vmem()],
         out_specs=vmem(),
         name="gram_block",
-    )(ranks, everyone)
+    )(everyone)
     tile = jnp.sum(lax.all_to_all(parts, "mus", 0, 0), axis=0)
     send = jnp.concatenate([tile[:, 0:128], summed[:, STACK : STACK + 128]], axis=1)
     tiles = lax.all_to_all(jnp.broadcast_to(send[None], (MUS,) + send.shape), "mus", 0, 0)
@@ -365,13 +367,13 @@
     half = BLOCK // 2
     kept = pl.pallas_call(
         place_kernel,
-        out_shape=jax.ShapeDtypeStruct((half, 2 * PAD + 128), f32),
-        in_specs=[smem(), vmem(), vmem()],
+        out_shape=jax.ShapeDtypeStruct((ROWS, half, 2 * PAD + 128), f32),
+        in_specs=[vmem(), vmem()],
         out_specs=vmem(),
         scratch_shapes=[pltpu.VMEM((BLOCK, 2 * PAD), f32)],
         name="place_rows",
-    )(ranks, tiles, tile)
-    mine = lax.all_to_all(jnp.broadcast_to(kept[None], (ROWS,) + kept.shape), "rows", 0, 0)
+    )(tiles, tile)
+    mine = lax.all_to_all(kept, "rows", 0, 0)
     theirs = lax.ppermute(mine, "mus", [(i, i ^ 1) for i in range(MUS)])
 
     coef, residual = pl.pallas_call(
@@ -380,7 +382,7 @@
             jax.ShapeDtypeStruct((OWN, TERMS), f32),
             jax.ShapeDtypeStruct((OWN, POSE_DEV), f32),
         ),
-        in_specs=[smem()] + [vmem()] * 5,
+        in_specs=[vmem()] * 3 + [pl.BlockSpec(memory_space=pl.ANY), vmem()],
         out_specs=(vmem(), vmem()),
         scratch_shapes=[
             pltpu.VMEM((PAD, 2 * PAD), f32),
@@ -390,9 +392,11 @@
         + [
             pltpu.VMEM((PAD, 128), f32),
             pltpu.VMEM((PAD, 128), f32),
+            pltpu.VMEM((PAD, POSE_DEV), f32),
+            pltpu.SemaphoreType.DMA(()),
         ],
         name="solve",
-    )(ranks, mine, theirs, everyone, basis, own)
+    )(mine, theirs, everyone, basis, own)
     return coef, residual
 
 

time: 122 us -> 121 us (level)
  blocking collectives: 63.8 us -> 84.6 us
  starting transfers between devices: 12.4 us -> 1 us
  waiting for transfers between devices: 11.6 us -> 2.47 us
    all_to_all x2 -> x3, blocking collectives: 34.1 us -> 54.9 us  [the longest x1 22.2 us: per_device(): mine = lax.all_to_all(kept, 'rows', 0, 0)]
    all_to_all x1 -> x0, starting transfers between devices: 11.3 us -> none  [per_device(): tile = jnp.sum(lax.all_to_all(parts, 'mus', 0, 0), axis=0)]
    all_to_all x1 -> x0, waiting for transfers between devices: 9.16 us -> none  [per_device(): tile = jnp.sum(lax.all_to_all(parts, 'mus', 0, 0), axis=0)]
  transfers between devices with their start and end apart: 2 -> 1, of which waited for: 2 -> 1; matrix products, arithmetic and copies ran while one was open for 0% -> 0% of each run, Pallas kernels for 0% -> 0%
where the time goes in v4:
time: 121 us; the launch traced here: 120 us
  blocking collectives  84.6 us (70%)
  Pallas kernels  29.5 us (24%)
  waiting for transfers between devices  2.47 us (2%)
  between operations  1.51 us (1%)
    all_to_all x1, blocking collectives, per_device(): mine = lax.all_to_all(kept, 'rows', 0, 0)  22.2 us
    all_to_all x1, blocking collectives, per_device(): tile = jnp.sum(lax.all_to_all(parts, 'mus', 0, 0), axis=0)  20.7 us
    pallas_call x1, Pallas kernels, per_device(): pl.pallas_call(solve_kernel, out_shape=(jax.ShapeDtypeStruct((OWN, TERMS)...  19.4 us
    all_to_all x1, blocking collectives, per_device(): summed = jnp.sum(lax.all_to_all(z, 'rows', 0, 0), axis=0)  18.1 us
    all_to_all x1, blocking collectives, per_device(): lax.all_to_all(jnp.broadcast_to(shared[None], (ROWS,) + shared.shape), 'r...  12 us
    all_to_all x1, blocking collectives, per_device(): lax.all_to_all(jnp.broadcast_to(send[None], (MUS,) + send.shape), 'mus',...  11.7 us
    pallas_call x1, Pallas kernels, per_device(): pl.pallas_call(local_kernel, out_shape=(jax.ShapeDtypeStruct((ROWS, 8, ST...  5.57 us
    ppermute x1, waiting for transfers between devices, per_device(): theirs = lax.ppermute(mine, 'mus', [(i, i ^ 1) for i in range(MUS)])  2.47 us
  transfers between devices with their start and end apart: 1, of which 1 were waited for; matrix products, arithmetic and copies ran while one was open for 0% of the time, Pallas kernels for 0%

profile of v4, /device:TPU:1, one launch (start us, length us, event | category | flops | bytes accessed | tf_op | source)
XLA Modules:
  0.0 120.2 jit_solution(2772699525453590524)
XLA Ops:
  1.3 5.6 %local_products.1 = (f32[16,8,1024]{2,1,0:T(8,128)}, f32[512,768]{1,0:T(8,128)}, f32[32,768]{1,0:T(8,128)}) custom-call(s32[1]{0:T(128)S(6)} %copy.6.seed_ref, s32[6,768]{1,0:T(8,128)} %ang_ref.1, f32[304,768]{1,0:T(8,128)} %len_ref.1, bf16[3,512,96]{2,1,0:T(8,128)(2,1)} %constant.4.clone.sel_ref), custom_call_target="tpu_custom_call" | custom-call | tf_op jit(solution)/shard_map/local_products/pallas_call | solution.py:333
  6.8 18.1 %all_to_all.25 = f32[16,8,1024]{2,1,0:T(8,128)S(1)} all-to-all(f32[16,8,1024]{2,1,0:T(8,128)} %get-tuple-element.5), channel_id=1, replica_groups=mesh['rows'=16,'mus'=16] {'rows'}, dimensions={0} | all-to-all | bytes 1048576 | tf_op jit(solution)/shard_map/all_to_all | solution.py:350
  25.0 12.0 %all_to_all.26.all_ref = f32[16,8,896]{2,1,0:T(8,128)} all-to-all(f32[16,8,896]{2,1,0:T(8,128)S(1)} %broadcast_in_dim.4), channel_id=1, replica_groups=mesh['rows'=16,'mus'=16] {'rows'}, dimensions={0} | all-to-all | bytes 917504 | tf_op jit(solution)/shard_map/all_to_all | solution.py:352
  37.0 2.3 %gram_block.1 = f32[16,8,256]{2,1,0:T(8,128)} custom-call(f32[16,8,896]{2,1,0:T(8,128)} %all_to_all.26.all_ref), custom_call_target="tpu_custom_call" | custom-call | tf_op jit(solution)/shard_map/gram_block/pallas_call | solution.py:356
  39.3 20.7 %all_to_all.27 = f32[16,8,256]{2,1,0:T(8,128)S(1)} all-to-all(f32[16,8,256]{2,1,0:T(8,128)} %gram_block.1), channel_id=1, replica_groups=mesh['rows'=16,'mus'=16] {'mus'}, dimensions={0} | all-to-all | bytes 262144 | tf_op jit(solution)/shard_map/all_to_all | solution.py:363
  60.0 0.0 copy-start.2
  60.1 11.7 %all_to_all.28.tiles_ref = f32[16,8,256]{2,1,0:T(8,128)} all-to-all(f32[16,8,256]{2,1,0:T(8,128)S(1)} %broadcast_in_dim.5), channel_id=1, replica_groups=mesh['rows'=16,'mus'=16] {'mus'}, dimensions={0} | all-to-all | bytes 262144 | tf_op jit(solution)/shard_map/all_to_all | solution.py:365
  71.8 0.0 copy-done.2
  71.8 2.2 %place_rows.1 = f32[16,16,1152]{2,1,0:T(8,128)} custom-call(f32[16,8,256]{2,1,0:T(8,128)} %all_to_all.28.tiles_ref, f32[8,256]{1,0:T(8,128)} %copy-done.2), custom_call_target="tpu_custom_call" | custom-call | tf_op jit(solution)/shard_map/place_rows/pallas_call | solution.py:368
  73.9 22.2 %all_to_all.29.mine_ref = f32[16,16,1152]{2,1,0:T(8,128)S(1)} all-to-all(f32[16,16,1152]{2,1,0:T(8,128)} %place_rows.1), channel_id=1, replica_groups=mesh['rows'=16,'mus'=16] {'rows'}, dimensions={0} | all-to-all | bytes 2359296 | tf_op jit(solution)/shard_map/all_to_all | solution.py:376
  96.1 0.0 copy-start
  96.1 1.0 collective-permute-start
  97.1 2.5 %collective-permute-done.theirs_ref = f32[16,16,1152]{2,1,0:T(8,128)S(1)} collective-permute-done((f32[16,16,1152]{2,1,0:T(8,128)S(1)}, f32[16,16,1152]{2,1,0:T(8,128)S(1)}, u32[]{:S(2)}, u32[]{:S(2)}) %collective-permute-start) | collective-permute-done | bytes 1179680 | tf_op jit(solution)/shard_map/ppermute | solution.py:377
  99.6 0.0 copy-start.1
  99.6 0.0 copy-done
  99.6 1.0 copy-done.1
  100.6 19.4 %solve.1 = (f32[19,462]{1,0:T(8,128)}, f32[19,768]{1,0:T(8,128)}) custom-call(f32[16,16,1152]{2,1,0:T(8,128)} %copy-done, f32[16,16,1152]{2,1,0:T(8,128)} %copy-done.1, f32[16,8,896]{2,1,0:T(8,128)} %all_to_all.26.all_ref, f32[512,768]{1,0:T(8,128)} %get-tuple-element.6.basis_hbm, f32[32,768]{1,0:T(8,128)} %get-tuple-element.7.own_ref), custom_call_target="tpu_custom_call" | custom-call | tf_op jit(solution)/shard_map/solve/pallas_call | solution.py:379
  (9 shorter events, 0.1 us)
Async XLA Ops:
  60.0 11.7 %copy-start.2 = (f32[8,256]{1,0:T(8,128)}, f32[8,256]{1,0:T(8,128)S(1)}, u32[]{:S(2)}) copy-start(f32[8,256]{1,0:T(8,128)S(1)} %reduce_sum.19.own_ref) | copy-start | bytes 24580
  96.1 3.5 %copy-start = (f32[16,16,1152]{2,1,0:T(8,128)}, f32[16,16,1152]{2,1,0:T(8,128)S(1)}, u32[]{:S(2)}) copy-start(f32[16,16,1152]{2,1,0:T(8,128)S(1)} %all_to_all.29.mine_ref) | copy-start | bytes 3538948
  96.1 3.5 %collective-permute-start = (f32[16,16,1152]{2,1,0:T(8,128)S(1)}, f32[16,16,1152]{2,1,0:T(8,128)S(1)}, u32[]{:S(2)}, u32[]{:S(2)}) collective-permute-start(f32[16,16,1152]{2,1,0:T(8,128)S(1)} %all_to_all.29.mine_ref), channel_id=1, source_target_pairs={{0,1},{1,0},{2,3},{3,2},{4,5},{5,4},{6,7},{7,6},{8,9},{9,8},{10,11... | collective-permute-start | bytes 3538952 | tf_op jit(solution)/shard_map/ppermute | solution.py:377
  99.6 1.0 copy-start.1

commit v5 on v4

--- a/solution.py
+++ b/solution.py
@@ -176,10 +176,11 @@
     half = BLOCK // 2
     core = lax.rem(lax.axis_index("mus"), 2)
     kept = row_ref[pl.ds(pl.multiple_of(core * half, half), half), :]
+    own = own_ref[...]
     for r in range(ROWS):
         out_ref[r, :, 0 : 2 * PAD] = kept
-        out_ref[r, 0:8, 2 * PAD :] = own_ref[:, 128:256]
-        out_ref[r, 8:half, 2 * PAD :] = jnp.zeros((half - 8, 128), f32)
+        out_ref[r, 0:8, 2 * PAD :] = own
+        out_ref[r, 8:half, 2 * PAD :] = jnp.zeros((half - 8, 256), f32)
 
 
 def solve_kernel(
@@ -221,7 +222,7 @@
                 r, :, STACK + lane : STACK + lane + BLOCK
             ]
             p_ref[at : at + 8, 0:BLOCK] = mine_ref[
-                r, 0:8, 2 * PAD + lane : 2 * PAD + lane + BLOCK
+                r, 0:8, 2 * PAD + 128 + lane : 2 * PAD + 128 + lane + BLOCK
             ]
     c_all = c_ref[...]
     lengths2 = c_all[PAD - 1 : PAD, :]
@@ -367,7 +368,7 @@
     half = BLOCK // 2
     kept = pl.pallas_call(
         place_kernel,
-        out_shape=jax.ShapeDtypeStruct((ROWS, half, 2 * PAD + 128), f32),
+        out_shape=jax.ShapeDtypeStruct((ROWS, half, 2 * PAD + 256), f32),
         in_specs=[vmem(), vmem()],
         out_specs=vmem(),
         scratch_shapes=[pltpu.VMEM((BLOCK, 2 * PAD), f32)],

time: 121 us -> 123 us (1.017)
  blocking collectives: 84.6 us -> 86 us
    all_to_all x1, blocking collectives: 22.2 us -> 23.6 us  [per_device(): mine = lax.all_to_all(kept, 'rows', 0, 0)]
where the time goes in v5:
time: 123 us; the launch traced here: 122 us
  blocking collectives  86 us (70%)
  Pallas kernels  29.7 us (24%)
  waiting for transfers between devices  2.66 us (2%)
  between operations  1.51 us (1%)
    all_to_all x1, blocking collectives, per_device(): mine = lax.all_to_all(kept, 'rows', 0, 0)  23.6 us
    all_to_all x1, blocking collectives, per_device(): tile = jnp.sum(lax.all_to_all(parts, 'mus', 0, 0), axis=0)  20.7 us
    pallas_call x1, Pallas kernels, per_device(): pl.pallas_call(solve_kernel, out_shape=(jax.ShapeDtypeStruct((OWN, TERMS)...  19.5 us
    all_to_all x1, blocking collectives, per_device(): summed = jnp.sum(lax.all_to_all(z, 'rows', 0, 0), axis=0)  18.1 us
    all_to_all x1, blocking collectives, per_device(): lax.all_to_all(jnp.broadcast_to(shared[None], (ROWS,) + shared.shape), 'r...  12 us
    all_to_all x1, blocking collectives, per_device(): lax.all_to_all(jnp.broadcast_to(send[None], (MUS,) + send.shape), 'mus',...  11.7 us
    pallas_call x1, Pallas kernels, per_device(): pl.pallas_call(local_kernel, out_shape=(jax.ShapeDtypeStruct((ROWS, 8, ST...  5.57 us
    ppermute x1, waiting for transfers between devices, per_device(): theirs = lax.ppermute(mine, 'mus', [(i, i ^ 1) for i in range(MUS)])  2.66 us
  transfers between devices with their start and end apart: 1, of which 1 were waited for; matrix products, arithmetic and copies ran while one was open for 0% of the time, Pallas kernels for 0%

profile of v5, /device:TPU:1, one launch (start us, length us, event | category | flops | bytes accessed | tf_op | source)
XLA Modules:
  0.0 122.1 jit_solution(17028305808231752068)
XLA Ops:
  1.3 5.6 %local_products.1 = (f32[16,8,1024]{2,1,0:T(8,128)}, f32[512,768]{1,0:T(8,128)}, f32[32,768]{1,0:T(8,128)}) custom-call(s32[1]{0:T(128)S(6)} %copy.6.seed_ref, s32[6,768]{1,0:T(8,128)} %ang_ref.1, f32[304,768]{1,0:T(8,128)} %len_ref.1, bf16[3,512,96]{2,1,0:T(8,128)(2,1)} %constant.4.clone.sel_ref), custom_call_target="tpu_custom_call" | custom-call | tf_op jit(solution)/shard_map/local_products/pallas_call | solution.py:334
  6.8 18.1 %all_to_all.25 = f32[16,8,1024]{2,1,0:T(8,128)S(1)} all-to-all(f32[16,8,1024]{2,1,0:T(8,128)} %get-tuple-element.5), channel_id=1, replica_groups=mesh['rows'=16,'mus'=16] {'rows'}, dimensions={0} | all-to-all | bytes 1048576 | tf_op jit(solution)/shard_map/all_to_all | solution.py:351
  25.0 12.0 %all_to_all.26.all_ref = f32[16,8,896]{2,1,0:T(8,128)} all-to-all(f32[16,8,896]{2,1,0:T(8,128)S(1)} %broadcast_in_dim.4), channel_id=1, replica_groups=mesh['rows'=16,'mus'=16] {'rows'}, dimensions={0} | all-to-all | bytes 917504 | tf_op jit(solution)/shard_map/all_to_all | solution.py:353
  37.0 2.3 %gram_block.1 = f32[16,8,256]{2,1,0:T(8,128)} custom-call(f32[16,8,896]{2,1,0:T(8,128)} %all_to_all.26.all_ref), custom_call_target="tpu_custom_call" | custom-call | tf_op jit(solution)/shard_map/gram_block/pallas_call | solution.py:357
  39.3 20.7 %all_to_all.27 = f32[16,8,256]{2,1,0:T(8,128)S(1)} all-to-all(f32[16,8,256]{2,1,0:T(8,128)} %gram_block.1), channel_id=1, replica_groups=mesh['rows'=16,'mus'=16] {'mus'}, dimensions={0} | all-to-all | bytes 262144 | tf_op jit(solution)/shard_map/all_to_all | solution.py:364
  60.0 0.0 copy-start.2
  60.1 11.7 %all_to_all.28.tiles_ref = f32[16,8,256]{2,1,0:T(8,128)} all-to-all(f32[16,8,256]{2,1,0:T(8,128)S(1)} %broadcast_in_dim.5), channel_id=1, replica_groups=mesh['rows'=16,'mus'=16] {'mus'}, dimensions={0} | all-to-all | bytes 262144 | tf_op jit(solution)/shard_map/all_to_all | solution.py:366
  71.8 0.0 copy-done.2
  71.8 2.3 %place_rows.1 = f32[16,16,1280]{2,1,0:T(8,128)} custom-call(f32[16,8,256]{2,1,0:T(8,128)} %all_to_all.28.tiles_ref, f32[8,256]{1,0:T(8,128)} %copy-done.2), custom_call_target="tpu_custom_call" | custom-call | tf_op jit(solution)/shard_map/place_rows/pallas_call | solution.py:369
  74.0 23.6 %all_to_all.29.mine_ref = f32[16,16,1280]{2,1,0:T(8,128)S(1)} all-to-all(f32[16,16,1280]{2,1,0:T(8,128)} %place_rows.1), channel_id=1, replica_groups=mesh['rows'=16,'mus'=16] {'rows'}, dimensions={0} | all-to-all | bytes 2621440 | tf_op jit(solution)/shard_map/all_to_all | solution.py:377
  97.6 0.0 copy-start
  97.7 1.1 collective-permute-start
  98.7 2.7 %collective-permute-done.theirs_ref = f32[16,16,1280]{2,1,0:T(8,128)S(1)} collective-permute-done((f32[16,16,1280]{2,1,0:T(8,128)S(1)}, f32[16,16,1280]{2,1,0:T(8,128)S(1)}, u32[]{:S(2)}, u32[]{:S(2)}) %collective-permute-start) | collective-permute-done | bytes 1310752 | tf_op jit(solution)/shard_map/ppermute | solution.py:378
  101.4 0.0 copy-start.1
  101.4 0.0 copy-done
  101.4 1.1 copy-done.1
  102.4 19.5 %solve.1 = (f32[19,462]{1,0:T(8,128)}, f32[19,768]{1,0:T(8,128)}) custom-call(f32[16,16,1280]{2,1,0:T(8,128)} %copy-done, f32[16,16,1280]{2,1,0:T(8,128)} %copy-done.1, f32[16,8,896]{2,1,0:T(8,128)} %all_to_all.26.all_ref, f32[512,768]{1,0:T(8,128)} %get-tuple-element.6.basis_hbm, f32[32,768]{1,0:T(8,128)} %get-tuple-element.7.own_ref), custom_call_target="tpu_custom_call" | custom-call | tf_op jit(solution)/shard_map/solve/pallas_call | solution.py:380
  (9 shorter events, 0.1 us)
Async XLA Ops:
  60.0 11.7 %copy-start.2 = (f32[8,256]{1,0:T(8,128)}, f32[8,256]{1,0:T(8,128)S(1)}, u32[]{:S(2)}) copy-start(f32[8,256]{1,0:T(8,128)S(1)} %reduce_sum.19.own_ref) | copy-start | bytes 24580
  97.6 3.7 %copy-start = (f32[16,16,1280]{2,1,0:T(8,128)}, f32[16,16,1280]{2,1,0:T(8,128)S(1)}, u32[]{:S(2)}) copy-start(f32[16,16,1280]{2,1,0:T(8,128)S(1)} %all_to_all.29.mine_ref) | copy-start | bytes 3932164
  97.7 3.7 %collective-permute-start = (f32[16,16,1280]{2,1,0:T(8,128)S(1)}, f32[16,16,1280]{2,1,0:T(8,128)S(1)}, u32[]{:S(2)}, u32[]{:S(2)}) collective-permute-start(f32[16,16,1280]{2,1,0:T(8,128)S(1)} %all_to_all.29.mine_ref), channel_id=1, source_target_pairs={{0,1},{1,0},{2,3},{3,2},{4,5},{5,4},{6,7},{7,6},{8,9},{9,8},{10,11... | collective-permute-start | bytes 3932168 | tf_op jit(solution)/shard_map/ppermute | solution.py:378
  101.4 1.1 copy-start.1
